TPU v7x, 128 devices: a whole 4x4x4 slice. The times are simulated.
128 devices in a mesh: section: 4 (over x), row: 32 (over z, y, core).
Axes of the slice: x: 4, y: 4, z: 4, core: 2. Of those that a mesh axis runs over, the one named last changes fastest.
Arguments:
- tokens: int32 [4, 64, 128], P(None, 'row'), may hold values from 0 to 32
- embed: bfloat16 [33, 768], replicated, may hold values from -6 to 6
- ln_gain: float32 [4, 768], P('section'), may hold values from 0.5 to 1.5
- w_qkv: bfloat16 [4, 768, 2304], P('section'), may hold values from -0.21875 to 0.21875
- w_out: bfloat16 [4, 768, 768], P('section'), may hold values from -0.21875 to 0.21875
- out_grad: bfloat16 [4, 64, 128, 768], P(None, 'row'), may hold values from -0.009887695 to 0.009887695
Outputs:
- grad_qkv: float32 [4, 768, 2304], P('section', 'row')
- grad_out: float32 [4, 768, 768], P('section', 'row')
- grad_gain: float32 [4, 768], P('section', 'row')
All inputs are finite; a program needn't handle non-finite values.
Results may differ from a plain program's by a relative error of at most 0.04.
Values may be sent and summed in bfloat16 or wider, within the bound.
A program may use at most 192 MiB of HBM per device.

v0:
```python
import math

import jax
import jax.numpy as jnp
from jax import lax
from jax.sharding import PartitionSpec as P

HEADS = 12
HEAD_DIM = 64
MICRO = 4


def shifted(value, axis, steps):
    count = lax.axis_size(axis)
    initial, last = (max(0, -steps), min(count, count - steps))
    return lax.ppermute(value, axis, [(source, source + steps) for source in range(initial, last)])


def norm_rows(x, gain):
    centred = x - jnp.mean(x, axis=-1, keepdims=True)
    spread = jnp.mean(centred * centred, axis=-1, keepdims=True)
    return (centred * lax.rsqrt(spread + 1e-05) * gain).astype(jnp.bfloat16)


def split_heads(qkv):
    parts = qkv.reshape(qkv.shape[0], qkv.shape[1], 3, HEADS, HEAD_DIM)
    return (parts[:, :, 0], parts[:, :, 1], parts[:, :, 2])


def project_rows(normed, wqkv):
    nrows, seq, width = normed.shape
    qkv = jnp.dot(normed.reshape(-1, width), wqkv, preferred_element_type=jnp.float32).astype(
        jnp.bfloat16
    )
    return qkv.reshape(nrows, seq, 3 * width)


def one_hot_table(tok_rows, vocab):
    flat = tok_rows.reshape(-1)
    return (jnp.arange(vocab, dtype=jnp.int32)[:, None] == flat[None, :]).astype(jnp.bfloat16)


def embed_rows(tok_rows, embed):
    table = one_hot_table(tok_rows, embed.shape[0])
    picked = lax.dot_general(
        table, embed, (((0,), (0,)), ((), ())), preferred_element_type=jnp.float32
    )
    return picked.reshape(tok_rows.shape[0], tok_rows.shape[1], embed.shape[1])


def layer_forward(x, gain, wqkv, wout, scale):
    nrows, seq, width = x.shape
    qkv = project_rows(norm_rows(x, gain), wqkv)
    query, keys, values = split_heads(qkv)
    logits = lax.psum(
        scale * jnp.einsum("rihd,rjhd->ihj", query, keys, preferred_element_type=jnp.float32), "row"
    )
    probs = jax.nn.softmax(logits, axis=-1).astype(jnp.bfloat16)
    mixed = jnp.einsum("ihj,rjhd->rihd", probs, values, preferred_element_type=jnp.float32).astype(
        jnp.bfloat16
    )
    mixed = mixed.reshape(-1, width)
    output = x + jnp.dot(mixed, wout, preferred_element_type=jnp.float32).reshape(nrows, seq, width)
    return (output, probs, qkv)


def soft_back(probs, d_probs):
    prob_f = probs.astype(jnp.float32)
    return (prob_f * (d_probs - jnp.sum(d_probs * prob_f, axis=-1, keepdims=True))).astype(
        jnp.bfloat16
    )


def layer_backward(x, gain, wqkv, wout, probs, qkv, upstream, scale):
    nrows, seq, width = x.shape
    normed, norm_back = jax.vjp(norm_rows, x, gain)
    query, keys, values = split_heads(qkv)
    mixed = jnp.einsum("ihj,rjhd->rihd", probs, values, preferred_element_type=jnp.float32).astype(
        jnp.bfloat16
    )
    flat_up = upstream.astype(jnp.bfloat16).reshape(-1, width)
    g_out = lax.dot_general(
        mixed.reshape(-1, width),
        flat_up,
        (((0,), (0,)), ((), ())),
        preferred_element_type=jnp.float32,
    )
    d_mixed = lax.dot_general(
        flat_up, wout, (((1,), (1,)), ((), ())), preferred_element_type=jnp.float32
    ).astype(jnp.bfloat16)
    d_mixed = d_mixed.reshape(nrows, seq, HEADS, HEAD_DIM)
    d_probs = lax.psum(
        jnp.einsum("rihd,rjhd->ihj", d_mixed, values, preferred_element_type=jnp.float32), "row"
    )
    d_logits = soft_back(probs, d_probs)
    d_values = jnp.einsum(
        "ihj,rihd->rjhd", probs, d_mixed, preferred_element_type=jnp.float32
    ).astype(jnp.bfloat16)
    d_query = (
        scale * jnp.einsum("ihj,rjhd->rihd", d_logits, keys, preferred_element_type=jnp.float32)
    ).astype(jnp.bfloat16)
    d_keys = (
        scale * jnp.einsum("ihj,rihd->rjhd", d_logits, query, preferred_element_type=jnp.float32)
    ).astype(jnp.bfloat16)
    d_qkv = jnp.stack([d_query, d_keys, d_values], axis=2).reshape(-1, 3 * width)
    g_qkv = lax.dot_general(
        normed.reshape(-1, width),
        d_qkv,
        (((0,), (0,)), ((), ())),
        preferred_element_type=jnp.float32,
    )
    d_normed = lax.dot_general(
        d_qkv, wqkv, (((1,), (1,)), ((), ())), preferred_element_type=jnp.float32
    ).astype(jnp.bfloat16)
    d_input, g_gain = norm_back(d_normed.reshape(nrows, seq, width))
    d_x = upstream + d_input
    return (d_x, g_qkv, g_out, g_gain)


def store_slot(buffer, value, index, valid):
    previous = lax.dynamic_index_in_dim(buffer, index, 0, keepdims=False)
    return lax.dynamic_update_index_in_dim(buffer, jnp.where(valid, value, previous), index, 0)


def local(tokens, embed, ln_gain, w_qkv, w_out, out_grad):
    n_section = lax.axis_size("section")
    n_row = lax.axis_size("row")
    section = lax.axis_index("section")
    rows_here = tokens.shape[1]
    seq = tokens.shape[2]
    width = embed.shape[1]
    scale = HEAD_DIM ** (-0.5) / math.sqrt(rows_here * n_row)
    gain = ln_gain[0]
    wqkv = w_qkv[0]
    wout = w_out[0]
    turns = MICRO + n_section - 1
    inputs_kept = jnp.zeros((MICRO, rows_here, seq, width), jnp.float32)
    probs_kept = jnp.zeros((MICRO, seq, HEADS, seq), jnp.bfloat16)
    qkv_kept = jnp.zeros((MICRO, rows_here, seq, 3 * width), jnp.bfloat16)
    incoming = jnp.zeros((rows_here, seq, width), jnp.float32)
    for turn in range(turns):
        micro = turn - section
        valid = (micro >= 0) & (micro < MICRO)
        index = jnp.clip(micro, 0, MICRO - 1)
        tok_now = lax.dynamic_index_in_dim(tokens, index, 0, keepdims=False)
        layer_in = jnp.where(section == 0, embed_rows(tok_now, embed), incoming)
        layer_out, probs, qkv = layer_forward(layer_in, gain, wqkv, wout, scale)
        inputs_kept = store_slot(inputs_kept, layer_in, index, valid)
        probs_kept = store_slot(probs_kept, probs, index, valid)
        qkv_kept = store_slot(qkv_kept, qkv, index, valid)
        if turn + 1 < turns:
            incoming = shifted(layer_out, "section", 1)
    acc_qkv = jnp.zeros((width, 3 * width), jnp.float32)
    acc_out = jnp.zeros((width, width), jnp.float32)
    acc_gain = jnp.zeros((width,), jnp.float32)
    returning = jnp.zeros((rows_here, seq, width), jnp.float32)
    for turn in range(turns):
        micro = turn - (n_section - 1 - section)
        valid = (micro >= 0) & (micro < MICRO)
        index = jnp.clip(micro, 0, MICRO - 1)
        arriving = lax.dynamic_index_in_dim(out_grad, index, 0, keepdims=False).astype(jnp.float32)
        upstream = jnp.where(section == n_section - 1, arriving, returning)
        layer_in = lax.dynamic_index_in_dim(inputs_kept, index, 0, keepdims=False)
        probs = lax.dynamic_index_in_dim(probs_kept, index, 0, keepdims=False)
        qkv = lax.dynamic_index_in_dim(qkv_kept, index, 0, keepdims=False)
        d_x, g_qkv, g_out, g_gain = layer_backward(
            layer_in, gain, wqkv, wout, probs, qkv, upstream, scale
        )
        acc_qkv = acc_qkv + jnp.where(valid, g_qkv, 0.0)
        acc_out = acc_out + jnp.where(valid, g_out, 0.0)
        acc_gain = acc_gain + jnp.where(valid, g_gain, 0.0)
        if turn + 1 < turns:
            returning = shifted(d_x, "section", -1)
    grad_qkv, grad_out, grad_gain = (
        lax.psum_scatter(acc_qkv[None], "row", scatter_dimension=1, tiled=True),
        lax.psum_scatter(acc_out[None], "row", scatter_dimension=1, tiled=True),
        lax.psum_scatter(acc_gain[None], "row", scatter_dimension=1, tiled=True),
    )
    return (grad_qkv, grad_out, grad_gain)


def solution(mesh):
    in_specs = (
        P(None, "row", None),
        P(),
        P("section", None),
        P("section", None, None),
        P("section", None, None),
        P(None, "row", None, None),
    )
    out_specs = (P("section", "row", None), P("section", "row", None), P("section", "row"))
    return jax.shard_map(local, mesh=mesh, in_specs=in_specs, out_specs=out_specs, check_vma=False)
```

profile of v0, /device:TPU:0, one launch (start us, length us, event | category | flops | bytes accessed | tf_op | source)
XLA Modules:
  0.0 2130.3 jit_solution(152075340100266287)
XLA Ops:
  14.3 3.7 broadcast_select_fusion
  20.4 3.5 reshape_reshape.21
  40.6 94.6 %all-reduce.16.cloned.1.call-done = f32[128,12,128]{0,2,1:T(8,128)} async-done(((f32[128,12,128]{0,2,1:T(8,128)}), f32[128,12,128]{0,2,1:T(8,128)}) %all-reduce.16.cloned.1.call-update) | async-done | bytes 786448 | tf_op jit(solution)/shard_map/psum | solution.py:55
  144.2 4.3 collective-permute-start
  160.9 3.9 collective-permute-done
  172.9 3.5 reshape_reshape.22
  176.5 2.9 fusion.515
  180.9 3.0 select_dynamic-update-slice_fusion.5
  183.9 103.1 %all-reduce.18.cloned.1.call-done = f32[128,12,128]{0,2,1:T(8,128)} async-done(((f32[128,12,128]{0,2,1:T(8,128)}), f32[128,12,128]{0,2,1:T(8,128)}) %all-reduce.18.cloned.1.call-update) | async-done | bytes 786448 | tf_op jit(solution)/shard_map/psum | solution.py:55
  295.2 3.6 collective-permute-start.1
  304.6 11.0 collective-permute-done.1
  323.8 3.5 reshape_reshape.23
  331.6 3.0 select_dynamic-update-slice_fusion.4
  334.5 102.2 %all-reduce.20.cloned.1.call-done = f32[128,12,128]{0,2,1:T(8,128)} async-done(((f32[128,12,128]{0,2,1:T(8,128)}), f32[128,12,128]{0,2,1:T(8,128)}) %all-reduce.20.cloned.1.call-update) | async-done | bytes 786448 | tf_op jit(solution)/shard_map/psum | solution.py:55
  445.0 3.6 collective-permute-start.2
  454.3 11.1 collective-permute-done.2
  473.6 3.5 reshape_reshape.24
  481.8 2.9 select_dynamic-update-slice_fusion.3
  484.8 101.8 %all-reduce.22.cloned.1.call-done = f32[128,12,128]{0,2,1:T(8,128)} async-done(((f32[128,12,128]{0,2,1:T(8,128)}), f32[128,12,128]{0,2,1:T(8,128)}) %all-reduce.22.cloned.1.call-update) | async-done | bytes 786448 | tf_op jit(solution)/shard_map/psum | solution.py:55
  594.8 3.6 collective-permute-start.3
  604.1 11.0 collective-permute-done.3
  623.3 3.5 reshape_reshape.25
  633.6 102.6 %all-reduce.24.cloned.1.call-done = f32[128,12,128]{0,2,1:T(8,128)} async-done(((f32[128,12,128]{0,2,1:T(8,128)}), f32[128,12,128]{0,2,1:T(8,128)}) %all-reduce.24.cloned.1.call-update) | async-done | bytes 786448 | tf_op jit(solution)/shard_map/psum | solution.py:55
  744.5 3.6 collective-permute-start.4
  753.9 11.0 collective-permute-done.4
  773.0 3.5 reshape_reshape.26
  785.1 100.8 %all-reduce.26.cloned.1.call-done = f32[128,12,128]{0,2,1:T(8,128)} async-done(((f32[128,12,128]{0,2,1:T(8,128)}), f32[128,12,128]{0,2,1:T(8,128)}) %all-reduce.26.cloned.1.call-update) | async-done | bytes 786448 | tf_op jit(solution)/shard_map/psum | solution.py:55
  894.2 3.6 collective-permute-start.5
  901.3 13.4 collective-permute-done.5
  922.8 3.5 reshape_reshape.27
  926.4 3.0 fusion.510
  937.5 6.4 constant_dynamic-slice_fusion.16
  945.1 4.7 fusion.495
  970.9 101.3 %all-reduce.40.cloned.1.call-done = (f32[128,12,128]{0,2,1:T(8,128)}, f32[128,12,128]{0,2,1:T(8,128)}) async-done(((f32[128,12,128]{0,2,1:T(8,128)}, f32[128,12,128]{0,2,1:T(8,128)}), (f32[128,12,128]{0,2,1:T(8,128)}, f32[128,12,128]{0,2,1:T(8,128)})) %all-reduce.40.cloned.1.call-update) | async-done | bytes 1572880 | tf_op jit(solution)/shard_map/psum | solution.py:55
  1078.8 2.9 fusion.173
  1081.7 3.1 fusion.172
  1096.0 16.1 collective-permute-done.6
  1125.7 99.7 %all-reduce.28.cloned.1.call-done = f32[128,12,128]{0,2,1:T(8,128)} async-done(((f32[128,12,128]{0,2,1:T(8,128)}), f32[128,12,128]{0,2,1:T(8,128)}) %all-reduce.28.cloned.1.call-update) | async-done | bytes 786448 | tf_op jit(solution)/shard_map/psum | solution.py:92
  1242.3 16.5 collective-permute-done.7
  1274.7 97.3 %all-reduce.30.cloned.1.call-done = f32[128,12,128]{0,2,1:T(8,128)} async-done(((f32[128,12,128]{0,2,1:T(8,128)}), f32[128,12,128]{0,2,1:T(8,128)}) %all-reduce.30.cloned.1.call-update) | async-done | bytes 786448 | tf_op jit(solution)/shard_map/psum | solution.py:92
  1372.0 2.9 fusion.169
  1375.0 3.0 fusion.168
  1391.6 13.9 collective-permute-done.8
  1421.1 97.5 %all-reduce.32.cloned.1.call-done = f32[128,12,128]{0,2,1:T(8,128)} async-done(((f32[128,12,128]{0,2,1:T(8,128)}), f32[128,12,128]{0,2,1:T(8,128)}) %all-reduce.32.cloned.1.call-update) | async-done | bytes 786448 | tf_op jit(solution)/shard_map/psum | solution.py:92
  1518.7 2.9 fusion.167
  1521.6 2.9 fusion.166
  1539.7 4.1 fusion.201
  1545.7 6.4 collective-permute-done.9
  1561.4 5.5 fusion.198
  1569.1 96.3 %all-reduce.34.cloned.1.call-done = f32[128,12,128]{0,2,1:T(8,128)} async-done(((f32[128,12,128]{0,2,1:T(8,128)}), f32[128,12,128]{0,2,1:T(8,128)}) %all-reduce.34.cloned.1.call-update) | async-done | bytes 786448 | tf_op jit(solution)/shard_map/psum | solution.py:92
  1680.4 4.0 fusion.195
  1686.3 12.2 collective-permute-done.10
  1707.8 5.5 fusion.192
  1715.4 96.2 %all-reduce.36.cloned.1.call-done = f32[128,12,128]{0,2,1:T(8,128)} async-done(((f32[128,12,128]{0,2,1:T(8,128)}), f32[128,12,128]{0,2,1:T(8,128)}) %all-reduce.36.cloned.1.call-update) | async-done | bytes 786448 | tf_op jit(solution)/shard_map/psum | solution.py:92
  1814.5 3.0 fusion.162
  1828.8 7.7 collective-permute-done.11
  1844.8 5.9 add_bitcast_fusion.1
  1851.2 5.5 fusion.189
  1856.7 4.0 fusion.186
  1862.9 86.1 %all-reduce.38.cloned.1.call-done = f32[128,12,128]{0,2,1:T(8,128)} async-done(((f32[128,12,128]{0,2,1:T(8,128)}), f32[128,12,128]{0,2,1:T(8,128)}) %all-reduce.38.cloned.1.call-update) | async-done | bytes 786448 | tf_op jit(solution)/shard_map/psum | solution.py:92
  1951.8 2.9 fusion.160
  1958.3 12.7 add_bitcast_fusion
  1975.7 66.2 %all-reduce = f32[1,768]{1,0:T(1,128)S(1)} all-reduce(f32[1,768]{1,0:T(1,128)S(1)} %reshape.1047), channel_id=4, replica_groups=mesh['section'=4,'row'=32] {'row'}, use_global_device_ids=true, to_apply=%region_84.85.clone | all-reduce | flops 768 | bytes 6144
  2042.5 81.2 %reduce-scatter.4.cloned.1.call-done = f32[1,24,2304]{2,1,0:T(8,128)} async-done(((f32[1,768,2304]{2,1,0:T(8,128)}), f32[1,24,2304]{2,1,0:T(8,128)}) %reduce-scatter.4.cloned.1.call-update) | async-done | bytes 221200 | tf_op jit(solution)/shard_map/reduce_scatter | solution.py:175
  (674 shorter events, 405.5 us)
Async XLA Ops:
  7.2 7.1 copy-start
  7.2 128.0 %all-reduce.16.cloned.1.call-start = ((), (), s32[]{:S(2)}) async-start(), calls=%async_computation.2 | async-start | bytes 1572864 | tf_op jit(solution)/shard_map/psum | solution.py:55
  28.0 258.9 %all-reduce.18.cloned.1.call-start = ((), (), s32[]{:S(2)}) async-start(), calls=%async_computation.3 | async-start | bytes 1572864 | tf_op jit(solution)/shard_map/psum | solution.py:55
  144.2 20.6 collective-permute-start
  156.7 8.0 copy-start.89
  180.6 256.1 %all-reduce.20.cloned.1.call-start = ((), (), s32[]{:S(2)}) async-start(), calls=%async_computation.4 | async-start | bytes 1572864 | tf_op jit(solution)/shard_map/psum | solution.py:55
  293.1 5.7 copy-start.25
  293.1 5.7 copy-start.88
  295.2 6.7 copy-start.95
  295.2 6.7 copy-start.124
  295.2 20.4 collective-permute-start.1
  301.9 13.7 copy-start.87
  331.5 255.0 %all-reduce.22.cloned.1.call-start = ((), (), s32[]{:S(2)}) async-start(), calls=%async_computation.5 | async-start | bytes 1572864 | tf_op jit(solution)/shard_map/psum | solution.py:55
  442.8 5.7 copy-start.27
  442.8 5.7 copy-start.91
  445.0 6.7 copy-start.96
  445.0 6.7 copy-start.125
  445.0 20.4 collective-permute-start.2
  451.7 13.7 copy-start.86
  481.3 254.9 %all-reduce.24.cloned.1.call-start = ((), (), s32[]{:S(2)}) async-start(), calls=%async_computation.6 | async-start | bytes 1572864 | tf_op jit(solution)/shard_map/psum | solution.py:55
  592.6 5.7 copy-start.29
  592.6 5.7 copy-start.92
  594.8 6.7 copy-start.97
  594.8 6.7 copy-start.126
  594.8 20.4 collective-permute-start.3
  601.5 13.7 copy-start.85
  631.0 254.9 %all-reduce.26.cloned.1.call-start = ((), (), s32[]{:S(2)}) async-start(), calls=%async_computation.7 | async-start | bytes 1572864 | tf_op jit(solution)/shard_map/psum | solution.py:55
  742.3 5.7 copy-start.31
  742.3 5.7 copy-start.93
  744.5 6.7 copy-start.98
  744.5 6.7 copy-start.127
  744.5 20.4 collective-permute-start.4
  751.2 13.7 copy-start.84
  780.7 291.5 %all-reduce.40.cloned.1.call-start = ((), (), s32[]{:S(2)}) async-start(), calls=%async_computation.16 | async-start | bytes 3145728 | tf_op jit(solution)/shard_map/psum | solution.py:55
  892.1 5.7 copy-start.51
  894.2 6.2 copy-start.99
  894.2 6.2 copy-start.128
  894.2 20.4 collective-permute-start.5
  900.4 14.2 copy-start.83
  932.0 13.1 copy-start.139
  933.6 11.4 copy-start.164
  965.2 260.1 %all-reduce.28.cloned.1.call-start = ((), (), s32[]{:S(2)}) async-start(), calls=%async_computation.8 | async-start | bytes 1572864 | tf_op jit(solution)/shard_map/psum | solution.py:92
  1090.7 21.4 %collective-permute-start.6 = (f32[2,128,768]{2,1,0:T(8,128)S(1)}, f32[2,128,768]{2,1,0:T(8,128)S(1)}, u32[]{:S(2)}, u32[]{:S(2)}) collective-permute-start(f32[2,128,768]{2,1,0:T(8,128)S(1)} %fusion.238), channel_id=1, source_target_pairs={{32,0},{64,32},{96,64},{33,1},{65,33},{97,65},{34,2},{66,34},{98,6... | collective-permute-start | bytes 2359304 | tf_op jit(solution)/shard_map/ppermute | solution.py:16
  1094.9 18.9 copy-start.2
  1121.1 250.9 %all-reduce.30.cloned.1.call-start = ((), (), s32[]{:S(2)}) async-start(), calls=%async_computation.9 | async-start | bytes 1572864 | tf_op jit(solution)/shard_map/psum | solution.py:92
  1237.3 21.5 %collective-permute-start.7 = (f32[2,128,768]{2,1,0:T(8,128)S(1)}, f32[2,128,768]{2,1,0:T(8,128)S(1)}, u32[]{:S(2)}, u32[]{:S(2)}) collective-permute-start(f32[2,128,768]{2,1,0:T(8,128)S(1)} %fusion.241), channel_id=1, source_target_pairs={{32,0},{64,32},{96,64},{33,1},{65,33},{97,65},{34,2},{66,34},{98,6... | collective-permute-start | bytes 2359304 | tf_op jit(solution)/shard_map/ppermute | solution.py:16
  1242.3 18.2 copy-start.3
  1267.9 250.8 %all-reduce.32.cloned.1.call-start = ((), (), s32[]{:S(2)}) async-start(), calls=%async_computation.10 | async-start | bytes 1572864 | tf_op jit(solution)/shard_map/psum | solution.py:92
  1384.1 5.5 copy-start.58
  1384.1 21.4 %collective-permute-start.8 = (f32[2,128,768]{2,1,0:T(8,128)S(1)}, f32[2,128,768]{2,1,0:T(8,128)S(1)}, u32[]{:S(2)}, u32[]{:S(2)}) collective-permute-start(f32[2,128,768]{2,1,0:T(8,128)S(1)} %fusion.244), channel_id=1, source_target_pairs={{32,0},{64,32},{96,64},{33,1},{65,33},{97,65},{34,2},{66,34},{98,6... | collective-permute-start | bytes 2359304 | tf_op jit(solution)/shard_map/ppermute | solution.py:16
  1391.6 15.5 copy-start.4
  1414.5 250.8 %all-reduce.34.cloned.1.call-start = ((), (), s32[]{:S(2)}) async-start(), calls=%async_computation.11 | async-start | bytes 1572864 | tf_op jit(solution)/shard_map/psum | solution.py:92
  1530.7 21.4 %collective-permute-start.9 = (f32[2,128,768]{2,1,0:T(8,128)S(1)}, f32[2,128,768]{2,1,0:T(8,128)S(1)}, u32[]{:S(2)}, u32[]{:S(2)}) collective-permute-start(f32[2,128,768]{2,1,0:T(8,128)S(1)} %fusion.247), channel_id=1, source_target_pairs={{32,0},{64,32},{96,64},{33,1},{65,33},{97,65},{34,2},{66,34},{98,6... | collective-permute-start | bytes 2359304 | tf_op jit(solution)/shard_map/ppermute | solution.py:16
  1545.7 8.1 copy-start.5
  1561.1 250.5 %all-reduce.36.cloned.1.call-start = ((), (), s32[]{:S(2)}) async-start(), calls=%async_computation.12 | async-start | bytes 1572864 | tf_op jit(solution)/shard_map/psum | solution.py:92
  1561.4 5.5 copy-start.68
  1677.2 21.3 collective-permute-start.10
  1686.3 13.8 copy-start.6
  1707.4 241.5 %all-reduce.38.cloned.1.call-start = ((), (), s32[]{:S(2)}) async-start(), calls=%async_computation.13 | async-start | bytes 1572864 | tf_op jit(solution)/shard_map/psum | solution.py:92
  1707.7 5.5 copy-start.69
  1823.7 12.8 collective-permute-start.11
  1826.9 10.5 copy-start.7
  1844.7 197.8 %reduce-scatter.6.cloned.1.call-start = ((), (), s32[]{:S(2)}) async-start(), calls=%async_computation.15 | async-start | bytes 2433024 | tf_op jit(solution)/shard_map/reduce_scatter | solution.py:176
  1850.7 272.9 %reduce-scatter.4.cloned.1.call-start = ((), (), s32[]{:S(2)}) async-start(), calls=%async_computation.14 | async-start | bytes 7299072 | tf_op jit(solution)/shard_map/reduce_scatter | solution.py:175
  (137 other events, 306.4 us)
Sparse Core Ops, SparseCore 0:
  28.2 106.9 all-reduce.15
  180.7 106.1 all-reduce.17
  331.6 105.0 all-reduce.19
  481.4 105.0 all-reduce.21
  631.1 105.0 all-reduce.23
  780.8 105.0 all-reduce.25
  965.3 106.8 all-reduce.39
  1121.2 104.0 all-reduce.27
  1268.0 103.9 all-reduce.29
  1414.6 104.0 all-reduce.31
  1561.3 104.0 all-reduce.33
  1707.6 104.0 all-reduce.35
  1844.8 104.0 all-reduce.37
  1953.0 79.1 reduce-scatter.5
  2036.4 87.2 reduce-scatter.3
where the time goes:
time: 2140 us; the launch traced here: 2130 us
  waiting for transfers between devices  1490 us (70%)
  matrix products  229 us (11%)
  local copies, waits for them, and re-layouts  197 us (9%)
  other arithmetic  93 us (4%)
  blocking collectives  66.2 us (3%)
  starting transfers between devices  33.7 us (2%)
    psum x7, waiting for transfers between devices, layer_forward(): lax.psum(scale * jnp.einsum('rihd,rjhd->ihj', query, keys, preferred_elem...  706 us
    psum x6, waiting for transfers between devices, layer_backward(): lax.psum(jnp.einsum('rihd,rjhd->ihj', d_mixed, values, preferred_element_...  573 us
    ppermute x12, waiting for transfers between devices, shifted(): lax.ppermute(value, axis, [(source, source + steps) for source in range(i...  134 us
    reduce_scatter x1, waiting for transfers between devices, local(): lax.psum_scatter(acc_qkv[None], 'row', scatter_dimension=1, tiled=True)  81.2 us
    unnamed x1, blocking collectives  66.2 us
  transfers between devices with their start and end apart: 27, of which 26 were waited for; matrix products, arithmetic and copies ran while one was open for 9% of the time, Pallas kernels for 0%

commit v1 on v0

v1 whole, which is shorter than its diff:
```python
import functools

import jax
import jax.numpy as jnp
from jax import lax
from jax.experimental import pallas as pl
from jax.experimental.pallas import tpu as pltpu
from jax.sharding import PartitionSpec as P

HEADS = 12
HEAD_DIM = 64
LAYERS = 4
PAIRS = HEADS // 2
WIDTH = HEADS * HEAD_DIM
SEQ = 128
MESH = pl.DeviceIdType.MESH
BF = jnp.bfloat16
F32 = jnp.float32


def dot(a, b, ca, cb):
    return lax.dot_general(a, b, (((ca,), (cb,)), ((), ())), preferred_element_type=F32)


def norm_parts(x):
    centred = x - jnp.mean(x, axis=-1, keepdims=True)
    spread = jnp.mean(centred * centred, axis=-1, keepdims=True)
    rstd = lax.rsqrt(spread + 1e-05)
    return centred * rstd, rstd


def kernel(
    n_row,
    scale,
    tok_ref,
    emb_ref,
    gain_ref,
    wqkv_hbm,
    wout_hbm,
    og_hbm,
    gq_hbm,
    go_hbm,
    wq,
    wo,
    xs,
    qkv,
    probs,
    mixed,
    part,
    recv,
    dlog,
    dyf,
    ogb,
    dmix,
    dqkv,
    hbuf,
    dhacc,
    gq,
    go,
    rs_send,
    rs_recv,
    ag_send,
    ag_recv,
    w_sem,
    og_sem,
    g_sem,
):
    sec = lax.axis_index("section")
    me = lax.axis_index("row")
    piece = part.shape[0] // n_row

    barrier = pltpu.get_barrier_semaphore()

    def greet(d, carry):
        peer = lax.rem(me + d, n_row)
        pl.semaphore_signal(barrier, inc=1, device_id=(sec, peer), device_id_type=MESH)
        return carry

    lax.fori_loop(1, n_row, greet, 0)

    for l in range(LAYERS):
        pltpu.make_async_copy(wqkv_hbm.at[l], wq.at[l], w_sem.at[0, l]).start()
        pltpu.make_async_copy(wout_hbm.at[l], wo.at[l], w_sem.at[1, l]).start()
    pltpu.make_async_copy(og_hbm.at[sec], ogb, og_sem).start()

    lane = lax.broadcasted_iota(jnp.int32, (1, SEQ), 1)
    low = (lane < HEAD_DIM).astype(F32).astype(BF)
    high = (lane >= HEAD_DIM).astype(F32).astype(BF)

    def rows_of(k):
        return pl.ds(pl.multiple_of(k * piece, 16), piece)

    def split_block(a0, a1):
        top = jnp.concatenate([a0 * low, a1 * low], axis=1)
        bottom = jnp.concatenate([a0 * high, a1 * high], axis=1)
        return jnp.concatenate([top, bottom], axis=0)

    def pair_scores(left, right, factor):
        for p in range(PAIRS):
            la, ra = left(p), right(p)
            out = dot(split_block(*la), jnp.concatenate(ra, axis=1), 1, 1)
            if factor is not None:
                out = factor * out
            part[pl.ds(2 * SEQ * p, 2 * SEQ), :] = out.astype(BF)

    def rs_copy(d):
        peer = lax.rem(me + d, n_row)
        return pltpu.make_async_remote_copy(
            src_ref=part.at[rows_of(peer)],
            dst_ref=recv.at[d],
            send_sem=rs_send.at[d],
            recv_sem=rs_recv.at[d],
            device_id=(sec, peer),
            device_id_type=MESH,
        )

    def start_reduce():
        def send(d, carry):
            rs_copy(d).start()
            return carry

        lax.fori_loop(1, n_row, send, 0)

    def finish_reduce():
        def take(d, total):
            rs_copy(d).wait_recv()
            return total + recv[d].astype(F32)

        return lax.fori_loop(1, n_row, take, part[rows_of(me), :].astype(F32))

    def ag_copy(buf, d):
        peer = lax.rem(me + d, n_row)
        return pltpu.make_async_remote_copy(
            src_ref=buf.at[rows_of(me)],
            dst_ref=buf.at[rows_of(me)],
            send_sem=ag_send.at[d],
            recv_sem=ag_recv.at[d],
            device_id=(sec, peer),
            device_id_type=MESH,
        )

    def start_gather(buf):
        def send(d, carry):
            ag_copy(buf, d).start()
            return carry

        lax.fori_loop(1, n_row, send, 0)

    def finish_gather(buf):
        def take(d, carry):
            ag_copy(buf, d).wait_recv()
            rs_copy(d).wait_send()
            ag_copy(buf, d).wait_send()
            return carry

        lax.fori_loop(1, n_row, take, 0)

    def halves(ref, base, p):
        cols = pl.ds(base + SEQ * p, SEQ)
        return ref[pl.ds(0, SEQ), cols], ref[pl.ds(SEQ, SEQ), cols]

    def beside(buf, p):
        return jnp.concatenate(
            [buf[pl.ds(2 * SEQ * p, SEQ), :], buf[pl.ds(2 * SEQ * p + SEQ, SEQ), :]], axis=1
        )

    def put_halves(ref, base, p, value):
        cols = pl.ds(base + SEQ * p, SEQ)
        ref[pl.ds(0, SEQ), cols] = value[:, :SEQ]
        ref[pl.ds(SEQ, SEQ), cols] = value[:, SEQ:]

    vocab = emb_ref.shape[0]
    ids = lax.broadcasted_iota(jnp.int32, (tok_ref.shape[0], vocab), 1)
    picks = (tok_ref[...] == ids).astype(F32).astype(BF)
    xs[0] = dot(picks, emb_ref[...], 1, 0)

    def forward(l, carry):
        x = xs[l]
        normal, _ = norm_parts(x)
        h = (normal * gain_ref[l]).astype(BF)
        pltpu.make_async_copy(wqkv_hbm.at[l], wq.at[l], w_sem.at[0, l]).wait()
        here = qkv.at[l]
        for n in range(3):
            cols = pl.ds(WIDTH * n, WIDTH)
            here[:, cols] = dot(h, wq[l, :, cols], 1, 0).astype(BF)
        pair_scores(lambda p: halves(here, 0, p), lambda p: halves(here, WIDTH, p), scale)

        @pl.when(l == 0)
        def _():
            pl.semaphore_wait(barrier, n_row - 1)

        start_reduce()
        logits = finish_reduce()
        shifted = jnp.exp(logits - jnp.max(logits, axis=-1, keepdims=True))
        own = shifted / jnp.sum(shifted, axis=-1, keepdims=True)
        probs_l = probs.at[l]
        probs_l[rows_of(me), :] = own.astype(BF)
        start_gather(probs_l)
        finish_gather(probs_l)
        mixed_l = mixed.at[l]
        for p in range(PAIRS):
            out = dot(beside(probs_l, p), split_block(*halves(here, 2 * WIDTH, p)), 1, 0)
            put_halves(mixed_l, 0, p, out.astype(BF))
        pltpu.make_async_copy(wout_hbm.at[l], wo.at[l], w_sem.at[1, l]).wait()

        @pl.when(l < LAYERS - 1)
        def _():
            xs[l + 1] = x + dot(mixed_l[...], wo[l], 1, 0)

        return carry

    lax.fori_loop(0, LAYERS, forward, 0)

    pltpu.make_async_copy(og_hbm.at[sec], ogb, og_sem).wait()
    dyf[...] = ogb[...].astype(F32)

    def backward(step, carry):
        l = LAYERS - 1 - step
        here = qkv.at[l]
        probs_l = probs.at[l]
        dyb = dyf[...].astype(BF)
        dmix[...] = dot(dyb, wo[l], 1, 1).astype(BF)
        pair_scores(lambda p: halves(dmix, 0, p), lambda p: halves(here, 2 * WIDTH, p), None)
        start_reduce()

        @pl.when(step > 0)
        def _():
            pltpu.make_async_copy(gq, gq_hbm.at[l], g_sem.at[0]).wait()
            pltpu.make_async_copy(go, go_hbm.at[l], g_sem.at[1]).wait()

        go[...] = dot(mixed[l], dyb, 0, 0).astype(BF)
        pltpu.make_async_copy(go, go_hbm.at[l], g_sem.at[1]).start()
        for p in range(PAIRS):
            rows = pl.ds(2 * SEQ * p, 2 * SEQ)
            out = dot(probs_l[rows, :], split_block(*halves(dmix, 0, p)), 0, 0)
            put_halves(dqkv, 2 * WIDTH, p, out.astype(BF))
        dprobs = finish_reduce()
        own = probs_l[rows_of(me), :].astype(F32)
        inner = jnp.sum(dprobs * own, axis=-1, keepdims=True)
        dlog[rows_of(me), :] = (own * (dprobs - inner)).astype(BF)
        start_gather(dlog)

        normal, rstd = norm_parts(xs[l])
        hbuf[...] = (normal * gain_ref[l]).astype(BF)
        vcols = pl.ds(2 * WIDTH, WIDTH)
        gq[:, vcols] = dot(hbuf[...], dqkv[:, vcols], 0, 0).astype(BF)
        dhacc[...] = dot(dqkv[:, vcols], wq[l, :, vcols], 1, 1)
        finish_gather(dlog)

        for p in range(PAIRS):
            out = dot(beside(dlog, p), split_block(*halves(here, WIDTH, p)), 1, 0)
            put_halves(dqkv, 0, p, (scale * out).astype(BF))
            rows = pl.ds(2 * SEQ * p, 2 * SEQ)
            out = dot(dlog[rows, :], split_block(*halves(here, 0, p)), 0, 0)
            put_halves(dqkv, WIDTH, p, (scale * out).astype(BF))
        qk = pl.ds(0, 2 * WIDTH)

        @pl.when(l > 0)
        def _():
            dh = dhacc[...] + dot(dqkv[:, qk], wq[l, :, qk], 1, 1)
            dn = dh.astype(BF).astype(F32) * gain_ref[l]
            first = jnp.mean(dn, axis=-1, keepdims=True)
            second = jnp.mean(dn * normal, axis=-1, keepdims=True)
            dyf[...] = dyf[...] + rstd * (dn - first - normal * second)

        for n in range(2):
            cols = pl.ds(WIDTH * n, WIDTH)
            gq[:, cols] = dot(hbuf[...], dqkv[:, cols], 0, 0).astype(BF)
        pltpu.make_async_copy(gq, gq_hbm.at[l], g_sem.at[0]).start()
        return carry

    lax.fori_loop(0, LAYERS, backward, 0)
    pltpu.make_async_copy(gq, gq_hbm.at[0], g_sem.at[0]).wait()
    pltpu.make_async_copy(go, go_hbm.at[0], g_sem.at[1]).wait()


def local(tokens, embed, ln_gain, w_qkv, w_out, out_grad):
    n_row = lax.axis_size("row")
    section = lax.axis_index("section")
    row = lax.axis_index("row")
    micro, rows_here, seq = tokens.shape
    vocab, width = embed.shape
    npos = rows_here * seq
    scale = HEAD_DIM ** (-0.5) / (rows_here * n_row) ** 0.5
    tok = lax.dynamic_index_in_dim(tokens, section, 0, keepdims=False).reshape(npos, 1)
    emb = jnp.pad(embed, ((0, -vocab % 16), (0, 0)))
    gains = lax.all_gather(ln_gain, "section", axis=0, tiled=False)
    wqkv = lax.all_gather(w_qkv, "section", axis=0, tiled=True)
    wout = lax.all_gather(w_out, "section", axis=0, tiled=True)
    flat = HEADS * seq
    vm, anyspace = pl.BlockSpec(memory_space=pltpu.VMEM), pl.BlockSpec(memory_space=pl.ANY)
    gq, go = pl.pallas_call(
        functools.partial(kernel, n_row, scale),
        out_shape=(
            jax.ShapeDtypeStruct((LAYERS, width, 3 * width), BF),
            jax.ShapeDtypeStruct((LAYERS, width, width), BF),
        ),
        in_specs=[vm, vm, vm, anyspace, anyspace, anyspace],
        out_specs=(anyspace, anyspace),
        scratch_shapes=[
            pltpu.VMEM((LAYERS, width, 3 * width), BF),
            pltpu.VMEM((LAYERS, width, width), BF),
            pltpu.VMEM((LAYERS, npos, width), F32),
            pltpu.VMEM((LAYERS, npos, 3 * width), BF),
            pltpu.VMEM((LAYERS, flat, seq), BF),
            pltpu.VMEM((LAYERS, npos, width), BF),
            pltpu.VMEM((flat, seq), BF),
            pltpu.VMEM((n_row, flat // n_row, seq), BF),
            pltpu.VMEM((flat, seq), BF),
            pltpu.VMEM((npos, width), F32),
            pltpu.VMEM((npos, width), BF),
            pltpu.VMEM((npos, width), BF),
            pltpu.VMEM((npos, 3 * width), BF),
            pltpu.VMEM((npos, width), BF),
            pltpu.VMEM((npos, width), F32),
            pltpu.VMEM((width, 3 * width), BF),
            pltpu.VMEM((width, width), BF),
            pltpu.SemaphoreType.DMA((n_row,)),
            pltpu.SemaphoreType.DMA((n_row,)),
            pltpu.SemaphoreType.DMA((n_row,)),
            pltpu.SemaphoreType.DMA((n_row,)),
            pltpu.SemaphoreType.DMA((2, LAYERS)),
            pltpu.SemaphoreType.DMA,
            pltpu.SemaphoreType.DMA((2,)),
        ],
        compiler_params=pltpu.CompilerParams(
            collective_id=0, has_side_effects=True, vmem_limit_bytes=64 * 1024 * 1024 - 1024 * 1024
        ),
    )(tok, emb, gains, wqkv, wout, out_grad.reshape(micro, npos, width))

    def reduced(g):
        g = lax.psum_scatter(g, "section", scatter_dimension=0, tiled=True)
        return lax.psum_scatter(g.astype(F32), "row", scatter_dimension=1, tiled=True)

    grad_qkv = reduced(gq)
    grad_out = reduced(go)
    own_rows = width // n_row
    w_own = lax.dynamic_slice_in_dim(w_qkv[0], row * own_rows, own_rows, 0).astype(F32)
    gain_own = lax.dynamic_slice_in_dim(ln_gain[0], row * own_rows, own_rows, 0)
    grad_gain = (jnp.sum(w_own * grad_qkv[0], axis=-1) / gain_own)[None]
    return (grad_qkv, grad_out, grad_gain)


def solution(mesh):
    in_specs = (
        P(None, "row", None),
        P(),
        P("section", None),
        P("section", None, None),
        P("section", None, None),
        P(None, "row", None, None),
    )
    out_specs = (P("section", "row", None), P("section", "row", None), P("section", "row"))
    return jax.shard_map(local, mesh=mesh, in_specs=in_specs, out_specs=out_specs, check_vma=False)
```

time: 2140 us -> 708 us (0.33)
  waiting for transfers between devices: 1490 us -> 521 us
  matrix products: 229 us -> 0 us
  local copies, waits for them, and re-layouts: 197 us -> 1.47 us
  Pallas kernels: 0 us -> 148 us
  other arithmetic: 93 us -> 10.1 us
  blocking collectives: 66.2 us -> 12.7 us
  starting transfers between devices: 33.7 us -> 0.24 us
    psum x13 -> x0, waiting for transfers between devices: 1280 us -> none  [the longest x7 706 us: layer_forward(): lax.psum(scale * jnp.einsum('rihd,rjhd->ihj', query, keys, preferred_elem...]
    reduce_scatter x2 -> x4, waiting for transfers between devices: 81.2 us -> 344 us  [the longest x2 174 us: reduced(): g = lax.psum_scatter(g, 'section', scatter_dimension=0, tiled=True)]
    dot_general x96 -> x0, matrix products: 229 us -> none  [the longest x7 41.2 us: layer_backward(): lax.dot_general(normed.reshape(-1, width), d_qkv, (((0,), (0,)), ((), ())...]
    all_gather x0 -> x2, waiting for transfers between devices: none -> 176 us  [the longest x1 134 us: local(): wqkv = lax.all_gather(w_qkv, 'section', axis=0, tiled=True)]
    pallas_call x0 -> x1, Pallas kernels: none -> 148 us  [local(): pl.pallas_call(functools.partial(kernel, n_row, scale), out_shape=(jax.Sh...]
    ppermute x12 -> x0, waiting for transfers between devices: 134 us -> none  [shifted(): lax.ppermute(value, axis, [(source, source + steps) for source in range(i...]
    unnamed x1 -> x0, blocking collectives: 66.2 us -> none
    convert_element_type x27 -> x0, local copies, waits for them, and re-layouts: 43.7 us -> none  [the longest x7 16.8 us: project_rows(): jnp.dot(normed.reshape(-1, width), wqkv, preferred_element_type=jnp.float32)]
  transfers between devices with their start and end apart: 27 -> 6, of which waited for: 26 -> 6; matrix products, arithmetic and copies ran while one was open for 9% -> 2% of each run, Pallas kernels for 0% -> 0%
where the time goes in v1:
time: 708 us
  waiting for transfers between devices  521 us (74%)
  Pallas kernels  148 us (21%)
  between operations  14.2 us (2%)
  blocking collectives  12.7 us (2%)
  other arithmetic  10.1 us (1%)
    reduce_scatter x2, waiting for transfers between devices, reduced(): g = lax.psum_scatter(g, 'section', scatter_dimension=0, tiled=True)  174 us
    reduce_scatter x2, waiting for transfers between devices, reduced(): lax.psum_scatter(g.astype(F32), 'row', scatter_dimension=1, tiled=True)  170 us
    pallas_call x1, Pallas kernels, local(): pl.pallas_call(functools.partial(kernel, n_row, scale), out_shape=(jax.Sh...  148 us
    all_gather x1, waiting for transfers between devices, local(): wqkv = lax.all_gather(w_qkv, 'section', axis=0, tiled=True)  134 us
    all_gather x1, waiting for transfers between devices, local(): wout = lax.all_gather(w_out, 'section', axis=0, tiled=True)  41.8 us
  transfers between devices with their start and end apart: 6, of which 6 were waited for; matrix products, arithmetic and copies ran while one was open for 2% of the time, Pallas kernels for 0%

profile of v1, /device:TPU:0, one launch (start us, length us, event | category | flops | bytes accessed | tf_op | source)
XLA Modules:
  0.0 707.7 jit_solution(13496473610544309798)
XLA Ops:
  7.2 0.0 copy-start
  7.2 0.0 copy-start.1
  7.2 0.0 copy-start.2
  7.2 0.0 all-gather.7.cloned.1.call-start
  7.2 0.7 all-gather.7.cloned.1.call-update
  7.9 0.0 all-gather.5.cloned.1.call-start
  8.0 0.7 all-gather.5.cloned.1.call-update
  8.7 0.0 reduce-scatter.5.cloned.1.call-start
  8.7 0.0 copy-done
  8.8 0.8 copy.10.tok_ref
  9.6 0.0 copy-done.1
  9.6 0.6 pad.4.emb_ref
  10.2 0.0 copy-done.2
  10.2 12.7 %all-gather.1.gain_ref = f32[4,1,768]{2,1,0:T(1,128)} all-gather(f32[1,1,768]{2,1,0:T(1,128)S(1)} %bitcast.6), channel_id=2, replica_groups=mesh['section'=4,'row'=32] {'section'}, dimensions={0}, use_global_device_ids=true | all-gather | bytes 15360 | tf_op jit(solution)/shard_map/all_gather | solution.py:287
  22.9 41.8 %all-gather.7.cloned.1.call-done.wout_hbm = bf16[4,768,768]{2,1,0:T(8,128)(2,1)} async-done(((bf16[1,768,768]{2,1,0:T(8,128)(2,1)}), bf16[4,768,768]{2,1,0:T(8,128)(2,1)}) %all-gather.7.cloned.1.call-update) | async-done | bytes 4718608 | tf_op jit(solution)/shard_map/all_gather | solution.py:289
  64.7 133.9 %all-gather.5.cloned.1.call-done.wqkv_hbm = bf16[4,768,2304]{2,1,0:T(8,128)(2,1)} async-done(((bf16[1,768,2304]{2,1,0:T(8,128)(2,1)}), bf16[4,768,2304]{2,1,0:T(8,128)(2,1)}) %all-gather.5.cloned.1.call-update) | async-done | bytes 14155792 | tf_op jit(solution)/shard_map/all_gather | solution.py:288
  198.7 147.6 %shard_map.85 = (bf16[4,768,2304]{2,1,0:T(8,128)(2,1)}, bf16[4,768,768]{2,1,0:T(8,128)(2,1)}) custom-call(s32[256,1]{1,0:T(8,128)} %copy.10.tok_ref, bf16[48,768]{1,0:T(8,128)(2,1)} %pad.4.emb_ref, f32[4,1,768]{2,1,0:T(1,128)} %all-gather.1.gain_ref, bf16[4,768,2304]{2,1,0:T(8,128)(2,1)} %all-gather.5.cloned.1.call-done.wqkv_hbm, ...), custom_call_target="tpu_custom_call" | custom-call | tf_op jit(solution)/shard_map/pallas_call | solution.py:292
  346.2 0.0 reduce-scatter.5.cloned.1.call-update
  346.3 0.0 reduce-scatter.9.cloned.1.call-start
  346.3 0.5 reduce-scatter.9.cloned.1.call-update
  346.8 0.0 reduce-scatter.7.cloned.1.call-start
  346.9 126.0 %reduce-scatter.5.cloned.1.call-done = bf16[1,768,2304]{2,1,0:T(8,128)(2,1)} async-done(((bf16[4,768,2304]{2,1,0:T(8,128)(2,1)}), bf16[1,768,2304]{2,1,0:T(8,128)(2,1)}) %reduce-scatter.5.cloned.1.call-update) | async-done | bytes 3538960 | tf_op jit(solution)/shard_map/reduce_scatter | solution.py:332
  472.9 5.4 convert_element_type.12
  478.3 0.0 reduce-scatter.7.cloned.1.call-update
  478.3 0.0 reduce-scatter.11.cloned.1.call-start
  478.4 47.6 %reduce-scatter.9.cloned.1.call-done = bf16[1,768,768]{2,1,0:T(8,128)(2,1)} async-done(((bf16[4,768,768]{2,1,0:T(8,128)(2,1)}), bf16[1,768,768]{2,1,0:T(8,128)(2,1)}) %reduce-scatter.9.cloned.1.call-update) | async-done | bytes 1179664 | tf_op jit(solution)/shard_map/reduce_scatter | solution.py:332
  526.0 2.9 convert_element_type.13
  528.9 0.0 reduce-scatter.11.cloned.1.call-update
  528.9 89.1 %reduce-scatter.7.cloned.1.call-done = f32[1,24,2304]{2,1,0:T(8,128)} async-done(((f32[1,768,2304]{2,1,0:T(8,128)}), f32[1,24,2304]{2,1,0:T(8,128)}) %reduce-scatter.7.cloned.1.call-update) | async-done | bytes 221200 | tf_op jit(solution)/shard_map/reduce_scatter | solution.py:333
  618.0 1.1 multiply_reduce_fusion
  619.2 0.6 fusion
  619.8 81.1 %reduce-scatter.11.cloned.1.call-done = f32[1,24,768]{2,1,0:T(8,128)} async-done(((f32[1,768,768]{2,1,0:T(8,128)}), f32[1,24,768]{2,1,0:T(8,128)}) %reduce-scatter.11.cloned.1.call-update) | async-done | bytes 73744 | tf_op jit(solution)/shard_map/reduce_scatter | solution.py:333
  (1 shorter events, 0.0 us)
Async XLA Ops:
  7.2 1.6 copy-start
  7.2 2.4 copy-start.1
  7.2 3.0 copy-start.2
  7.2 57.5 %all-gather.7.cloned.1.call-start = ((), (), s32[]{:S(2)}) async-start(), calls=%async_computation.5 | async-start | bytes 5898240 | tf_op jit(solution)/shard_map/all_gather | solution.py:289
  7.9 190.7 %all-gather.5.cloned.1.call-start = ((), (), s32[]{:S(2)}) async-start(), calls=%async_computation.4 | async-start | bytes 17694720 | tf_op jit(solution)/shard_map/all_gather | solution.py:288
  8.7 464.2 %reduce-scatter.5.cloned.1.call-start = ((), (), s32[]{:S(2)}) async-start(), calls=%async_computation.6 | async-start | bytes 17694720 | tf_op jit(solution)/shard_map/reduce_scatter | solution.py:332
  346.3 179.7 %reduce-scatter.9.cloned.1.call-start = ((), (), s32[]{:S(2)}) async-start(), calls=%async_computation.8 | async-start | bytes 5898240 | tf_op jit(solution)/shard_map/reduce_scatter | solution.py:332
  346.8 271.2 %reduce-scatter.7.cloned.1.call-start = ((), (), s32[]{:S(2)}) async-start(), calls=%async_computation.7 | async-start | bytes 7299072 | tf_op jit(solution)/shard_map/reduce_scatter | solution.py:333
  478.3 222.6 %reduce-scatter.11.cloned.1.call-start = ((), (), s32[]{:S(2)}) async-start(), calls=%async_computation.9 | async-start | bytes 2433024 | tf_op jit(solution)/shard_map/reduce_scatter | solution.py:333
Sparse Core Ops, SparseCore 0:
  9.7 55.0 all-gather.6
  66.4 132.2 all-gather.4
  346.4 126.4 reduce-scatter.4
  475.1 50.8 reduce-scatter.8
  530.2 87.7 reduce-scatter.6
  622.0 78.7 reduce-scatter.10

commit v2 on v1

--- a/solution.py
+++ b/solution.py
@@ -13,6 +13,11 @@
 PAIRS = HEADS // 2
 WIDTH = HEADS * HEAD_DIM
 SEQ = 128
+SIDE = 4
+OUT, VAL, QRY, KEY = 0, 1, 2, 3
+CHUNKS = 6
+CHUNKS_FIRST = 2
+QUARTER = WIDTH // 4
 MESH = pl.DeviceIdType.MESH
 BF = jnp.bfloat16
 F32 = jnp.float32
@@ -38,10 +43,11 @@
     wqkv_hbm,
     wout_hbm,
     og_hbm,
-    gq_hbm,
-    go_hbm,
-    wq,
-    wo,
+    gq_ref,
+    go_ref,
+    wcat,
+    gains,
+    tab,
     xs,
     qkv,
     probs,
@@ -55,19 +61,58 @@
     dqkv,
     hbuf,
     dhacc,
-    gq,
-    go,
+    grad,
+    pairbuf,
+    line1,
+    sum1,
+    line2,
+    xout,
+    xin,
+    fin,
     rs_send,
     rs_recv,
     ag_send,
     ag_recv,
     w_sem,
     og_sem,
-    g_sem,
+    tab_send,
+    tab_recv,
+    gain_send,
+    gain_recv,
+    ring_send,
+    ring_recv,
+    twin_send,
+    twin_recv,
+    pair_send,
+    pair_recv,
+    c1_send,
+    c1_recv,
+    c2_send,
+    c2_recv,
+    x_send,
+    x_recv,
 ):
     sec = lax.axis_index("section")
     me = lax.axis_index("row")
     piece = part.shape[0] // n_row
+    core = lax.rem(me, 2)
+    partner = me + 1 - 2 * core
+    chip = me // 2
+    zc = chip // SIDE
+    yc = lax.rem(chip, SIDE)
+
+    def row_at(z, y):
+        return (z * SIDE + y) * 2 + core
+
+    local_qkv = pltpu.make_async_copy(
+        wqkv_hbm.at[0], wcat.at[sec, :, pl.ds(0, 3 * WIDTH)], w_sem.at[0]
+    )
+    local_out = pltpu.make_async_copy(
+        wout_hbm.at[0], wcat.at[sec, :, pl.ds(3 * WIDTH, WIDTH)], w_sem.at[1]
+    )
+    local_qkv.start()
+    local_out.start()
+    pltpu.make_async_copy(og_hbm.at[sec], ogb, og_sem).start()
 
     barrier = pltpu.get_barrier_semaphore()
 
@@ -77,15 +122,148 @@
         return carry
 
     lax.fori_loop(1, n_row, greet, 0)
-
-    for l in range(LAYERS):
-        pltpu.make_async_copy(wqkv_hbm.at[l], wq.at[l], w_sem.at[0, l]).start()
-        pltpu.make_async_copy(wout_hbm.at[l], wo.at[l], w_sem.at[1, l]).start()
-    pltpu.make_async_copy(og_hbm.at[sec], ogb, og_sem).start()
+    for d in range(1, LAYERS):
+        pl.semaphore_signal(
+            barrier, inc=1, device_id=(lax.rem(sec + d, LAYERS), me), device_id_type=MESH
+        )
 
     lane = lax.broadcasted_iota(jnp.int32, (1, SEQ), 1)
     low = (lane < HEAD_DIM).astype(F32).astype(BF)
     high = (lane >= HEAD_DIM).astype(F32).astype(BF)
+
+    gains[sec] = gain_ref[...]
+    vocab = emb_ref.shape[0]
+    ids = lax.broadcasted_iota(jnp.int32, (tok_ref.shape[0], vocab), 1)
+    picks = (tok_ref[...] == ids).astype(F32).astype(BF)
+    xs[0] = dot(picks, emb_ref[...], 1, 0)
+
+    local_qkv.wait()
+
+    @pl.when(sec == 0)
+    def _():
+        normal, _ = norm_parts(emb_ref[...].astype(F32))
+        h = (normal * gain_ref[...]).astype(BF)
+        for n in range(3):
+            cols = pl.ds(WIDTH * n, WIDTH)
+            tab[:, cols] = dot(h, wcat[0, :, cols], 1, 0).astype(BF)
+
+    local_out.wait()
+    pl.semaphore_wait(barrier, n_row - 1 + LAYERS - 1)
+
+    def tab_copy(t):
+        return pltpu.make_async_remote_copy(
+            src_ref=tab,
+            dst_ref=tab,
+            send_sem=tab_send.at[t],
+            recv_sem=tab_recv,
+            device_id=(t, me),
+            device_id_type=MESH,
+        )
+
+    @pl.when(sec == 0)
+    def _():
+        for t in range(1, LAYERS):
+            tab_copy(t).start()
+
+    def gain_copy(d):
+        return pltpu.make_async_remote_copy(
+            src_ref=gain_ref,
+            dst_ref=gains.at[sec],
+            send_sem=gain_send.at[d],
+            recv_sem=gain_recv.at[d],
+            device_id=(lax.rem(sec + d, LAYERS), me),
+            device_id_type=MESH,
+        )
+
+    for d in range(1, LAYERS):
+        gain_copy(d).start()
+
+    def flow(l, d, k, who, first):
+        rows = QUARTER // (CHUNKS_FIRST if first else CHUNKS)
+        start = who * (2 * QUARTER) + d * QUARTER + k * rows
+        span = pl.ds(pl.multiple_of(start, 16), rows)
+        if first:
+            return wcat.at[0, span, pl.ds(3 * WIDTH, WIDTH)]
+        return wcat.at[l, span]
+
+    def place(l, d):
+        return lax.rem(sec - l + LAYERS, LAYERS) if d == 0 else lax.rem(l - sec + LAYERS, LAYERS)
+
+    def ring_copy(l, d, k, first):
+        step = 1 if d == 0 else LAYERS - 1
+        ref = flow(l, d, k, core, first)
+        return pltpu.make_async_remote_copy(
+            src_ref=ref,
+            dst_ref=ref,
+            send_sem=ring_send.at[l, d, k],
+            recv_sem=ring_recv.at[l, d, k],
+            device_id=(lax.rem(sec + step, LAYERS), me),
+            device_id_type=MESH,
+        )
+
+    def twin_copy(l, d, k, who, first):
+        ref = flow(l, d, k, who, first)
+        return pltpu.make_async_remote_copy(
+            src_ref=ref,
+            dst_ref=ref,
+            send_sem=twin_send.at[l, d, k],
+            recv_sem=twin_recv.at[l, d, k],
+            device_id=(sec, partner),
+            device_id_type=MESH,
+        )
+
+    def launch_flow(l, first=False):
+        chunks = CHUNKS_FIRST if first else CHUNKS
+
+        @pl.when(sec == l)
+        def _():
+            for k in range(chunks):
+                for d in range(2):
+                    ring_copy(l, d, k, first).start()
+
+    def pump(l, slot, first=False):
+        chunks = CHUNKS_FIRST if first else CHUNKS
+        for d in range(2):
+            at = place(l, d)
+            k = slot - at
+
+            @pl.when((at > 0) & (k >= 0) & (k < chunks))
+            def _():
+                ring_copy(l, d, k, first).wait_recv()
+
+                @pl.when(at < LAYERS - 1)
+                def _():
+                    ring_copy(l, d, k, first).start()
+
+                twin_copy(l, d, k, core, first).start()
+
+    def settle(l, first=False):
+        chunks = CHUNKS_FIRST if first else CHUNKS
+
+        @pl.when(sec != l)
+        def _():
+            for k in range(chunks):
+                for d in range(2):
+                    twin_copy(l, d, k, 1 - core, first).wait_recv()
+
+    def drain(l, first=False):
+        chunks = CHUNKS_FIRST if first else CHUNKS
+
+        def one(k, carry):
+            for d in range(2):
+                at = place(l, d)
+
+                @pl.when(at < LAYERS - 1)
+                def _():
+                    ring_copy(l, d, k, first).wait_send()
+
+                @pl.when(at > 0)
+                def _():
+                    twin_copy(l, d, k, core, first).wait_send()
+
+            return carry
+
+        lax.fori_loop(0, chunks, one, 0)
 
     def rows_of(k):
         return pl.ds(pl.multiple_of(k * piece, 16), piece)
@@ -169,43 +347,188 @@
         ref[pl.ds(0, SEQ), cols] = value[:, :SEQ]
         ref[pl.ds(SEQ, SEQ), cols] = value[:, SEQ:]
 
-    vocab = emb_ref.shape[0]
-    ids = lax.broadcasted_iota(jnp.int32, (tok_ref.shape[0], vocab), 1)
-    picks = (tok_ref[...] == ids).astype(F32).astype(BF)
-    xs[0] = dot(picks, emb_ref[...], 1, 0)
+    own_rows = WIDTH // n_row
+
+    def put_grad(u, value):
+        for r in range(n_row):
+            q = r // 2
+            grad[u, r % 2, q // SIDE, q % SIDE] = value[own_rows * r : own_rows * (r + 1)].astype(BF)
+
+    def pair_copy(u, par):
+        return pltpu.make_async_remote_copy(
+            src_ref=grad.at[u, 1 - core],
+            dst_ref=pairbuf.at[par, u],
+            send_sem=pair_send.at[u],
+            recv_sem=pair_recv.at[par, u],
+            device_id=(sec, partner),
+            device_id_type=MESH,
+        )
+
+    def y_first(u):
+        return u % 2 == 0
+
+    def c1_copy(u, par, d):
+        if y_first(u):
+            y = lax.rem(yc + d, SIDE)
+            src, peer = grad.at[u, core, :, y], row_at(zc, y)
+        else:
+            z = lax.rem(zc + d, SIDE)
+            src, peer = grad.at[u, core, z], row_at(z, yc)
+        return pltpu.make_async_remote_copy(
+            src_ref=src,
+            dst_ref=line1.at[par, u, d - 1],
+            send_sem=c1_send.at[u, d - 1],
+            recv_sem=c1_recv.at[par, u, d - 1],
+            device_id=(sec, peer),
+            device_id_type=MESH,
+        )
+
+    def c2_copy(u, par, d):
+        if y_first(u):
+            at = lax.rem(zc + d, SIDE)
+            peer = row_at(at, yc)
+        else:
+            at = lax.rem(yc + d, SIDE)
+            peer = row_at(zc, at)
+        return pltpu.make_async_remote_copy(
+            src_ref=sum1.at[par, u, at],
+            dst_ref=line2.at[par, u, d - 1],
+            send_sem=c2_send.at[u, d - 1],
+            recv_sem=c2_recv.at[par, u, d - 1],
+            device_id=(sec, peer),
+            device_id_type=MESH,
+        )
+
+    def x_copy(u, t):
+        owner = LAYERS - 1 - t
+        return pltpu.make_async_remote_copy(
+            src_ref=xout.at[u],
+            dst_ref=xin.at[u, lax.rem(sec - owner + LAYERS - 1 + LAYERS, LAYERS)],
+            send_sem=x_send.at[u],
+            recv_sem=x_recv.at[u, lax.rem(sec - owner + LAYERS - 1 + LAYERS, LAYERS)],
+            device_id=(owner, me),
+            device_id_type=MESH,
+        )
+
+    def stage_pair(u, t):
+        pair_copy(u, t % 2).start()
+
+    def stage_one(u, t):
+        par = t % 2
+        pair_copy(u, par).wait_recv()
+        pair_copy(u, par).wait_send()
+        for z in range(SIDE):
+            both = grad[u, core, z].astype(F32) + pairbuf[par, u, z].astype(F32)
+            grad[u, core, z] = both.astype(BF)
+        for d in range(1, SIDE):
+            c1_copy(u, par, d).start()
+
+    def stage_two(u, t):
+        par = t % 2
+        for d in range(1, SIDE):
+            c1_copy(u, par, d).wait_recv()
+            c1_copy(u, par, d).wait_send()
+        for k in range(SIDE):
+            own = grad[u, core, k, yc] if y_first(u) else grad[u, core, zc, k]
+            total = own.astype(F32)
+            for d in range(SIDE - 1):
+                total = total + line1[par, u, d, k].astype(F32)
+            sum1[par, u, k] = total.astype(BF)
+        for d in range(1, SIDE):
+            c2_copy(u, par, d).start()
+
+    def stage_three(u, t):
+        par = t % 2
+        owner = LAYERS - 1 - t
+        for d in range(1, SIDE):
+            c2_copy(u, par, d).wait_recv()
+            c2_copy(u, par, d).wait_send()
+        total = sum1[par, u, zc if y_first(u) else yc].astype(F32)
+        for d in range(SIDE - 1):
+            total = total + line2[par, u, d].astype(F32)
+
+        @pl.when((t > 0) & (sec != owner + 1))
+        def _():
+            x_copy(u, t - 1).wait_send()
+
+        @pl.when(sec == owner)
+        def _():
+            fin[u] = total
+
+        @pl.when(sec != owner)
+        def _():
+            xout[u] = total.astype(BF)
+            x_copy(u, t).start()
+
+    launch_flow(0, True)
+    launch_flow(1)
 
     def forward(l, carry):
-        x = xs[l]
-        normal, _ = norm_parts(x)
-        h = (normal * gain_ref[l]).astype(BF)
-        pltpu.make_async_copy(wqkv_hbm.at[l], wq.at[l], w_sem.at[0, l]).wait()
         here = qkv.at[l]
-        for n in range(3):
-            cols = pl.ds(WIDTH * n, WIDTH)
-            here[:, cols] = dot(h, wq[l, :, cols], 1, 0).astype(BF)
+
+        @pl.when(l == 0)
+        def _():
+            @pl.when(sec > 0)
+            def _():
+                tab_copy(0).wait_recv()
+
+            for d in range(1, LAYERS):
+                gain_copy(d).wait_recv()
+            for n in range(3):
+                cols = pl.ds(WIDTH * n, WIDTH)
+                here[:, cols] = dot(picks, tab[:, cols], 1, 0).astype(BF)
+
+        @pl.when(l > 0)
+        def _():
+            settle(l)
+            normal, _ = norm_parts(xs[l])
+            h = (normal * gains[l]).astype(BF)
+            for n in range(3):
+                cols = pl.ds(WIDTH * n, WIDTH)
+                here[:, cols] = dot(h, wcat[l, :, cols], 1, 0).astype(BF)
+
         pair_scores(lambda p: halves(here, 0, p), lambda p: halves(here, WIDTH, p), scale)
+        start_reduce()
 
         @pl.when(l == 0)
         def _():
-            pl.semaphore_wait(barrier, n_row - 1)
-
-        start_reduce()
+            for slot in range(1, CHUNKS_FIRST + 3):
+                pump(0, slot, True)
+
+        @pl.when((l > 0) & (l < LAYERS - 1))
+        def _():
+            launch_flow(l + 1)
+
+        @pl.when(l < LAYERS - 1)
+        def _():
+            for slot in range(1, 5):
+                pump(l + 1, slot)
+
         logits = finish_reduce()
         shifted = jnp.exp(logits - jnp.max(logits, axis=-1, keepdims=True))
         own = shifted / jnp.sum(shifted, axis=-1, keepdims=True)
         probs_l = probs.at[l]
         probs_l[rows_of(me), :] = own.astype(BF)
         start_gather(probs_l)
+
+        @pl.when(l < LAYERS - 1)
+        def _():
+            for slot in range(5, CHUNKS + 3):
+                pump(l + 1, slot)
+
         finish_gather(probs_l)
         mixed_l = mixed.at[l]
         for p in range(PAIRS):
             out = dot(beside(probs_l, p), split_block(*halves(here, 2 * WIDTH, p)), 1, 0)
             put_halves(mixed_l, 0, p, out.astype(BF))
-        pltpu.make_async_copy(wout_hbm.at[l], wo.at[l], w_sem.at[1, l]).wait()
+
+        @pl.when(l == 0)
+        def _():
+            settle(0, True)
 
         @pl.when(l < LAYERS - 1)
         def _():
-            xs[l + 1] = x + dot(mixed_l[...], wo[l], 1, 0)
+            xs[l + 1] = xs[l] + dot(mixed_l[...], wcat[l, :, pl.ds(3 * WIDTH, WIDTH)], 1, 0)
 
         return carry
 
@@ -213,23 +536,52 @@
 
     pltpu.make_async_copy(og_hbm.at[sec], ogb, og_sem).wait()
     dyf[...] = ogb[...].astype(F32)
+
+    def reduce_window(step):
+        def previous():
+            t = step - 1
+            for u, n in ((QRY, 0), (KEY, 1)):
+                put_grad(u, dot(hbuf[...], dqkv[:, pl.ds(WIDTH * n, WIDTH)], 0, 0))
+                stage_pair(u, t)
+            for u in (OUT, VAL):
+                stage_one(u, t)
+
+        def older():
+            t = step - 2
+            for u in (OUT, VAL):
+                stage_three(u, t)
+            for u in (QRY, KEY):
+                stage_two(u, t)
+
+        return older, previous
+
+    def gather_window(step):
+        def previous():
+            t = step - 1
+            for u in (OUT, VAL):
+                stage_two(u, t)
+            for u in (QRY, KEY):
+                stage_one(u, t)
+
+        def older():
+            t = step - 2
+            for u in (QRY, KEY):
+                stage_three(u, t)
+
+        return previous, older
 
     def backward(step, carry):
         l = LAYERS - 1 - step
         here = qkv.at[l]
         probs_l = probs.at[l]
         dyb = dyf[...].astype(BF)
-        dmix[...] = dot(dyb, wo[l], 1, 1).astype(BF)
+        dmix[...] = dot(dyb, wcat[l, :, pl.ds(3 * WIDTH, WIDTH)], 1, 1).astype(BF)
         pair_scores(lambda p: halves(dmix, 0, p), lambda p: halves(here, 2 * WIDTH, p), None)
         start_reduce()
 
-        @pl.when(step > 0)
-        def _():
-            pltpu.make_async_copy(gq, gq_hbm.at[l], g_sem.at[0]).wait()
-            pltpu.make_async_copy(go, go_hbm.at[l], g_sem.at[1]).wait()
-
-        go[...] = dot(mixed[l], dyb, 0, 0).astype(BF)
-        pltpu.make_async_copy(go, go_hbm.at[l], g_sem.at[1]).start()
+        older, previous = reduce_window(step)
+        pl.when(step >= 2)(older)
+        pl.when(step >= 1)(previous)
         for p in range(PAIRS):
             rows = pl.ds(2 * SEQ * p, 2 * SEQ)
             out = dot(probs_l[rows, :], split_block(*halves(dmix, 0, p)), 0, 0)
@@ -241,10 +593,20 @@
         start_gather(dlog)
 
         normal, rstd = norm_parts(xs[l])
-        hbuf[...] = (normal * gain_ref[l]).astype(BF)
+        hbuf[...] = (normal * gains[l]).astype(BF)
         vcols = pl.ds(2 * WIDTH, WIDTH)
-        gq[:, vcols] = dot(hbuf[...], dqkv[:, vcols], 0, 0).astype(BF)
-        dhacc[...] = dot(dqkv[:, vcols], wq[l, :, vcols], 1, 1)
+        previous, older = gather_window(step)
+        pl.when(step >= 1)(previous)
+        put_grad(OUT, dot(mixed[l], dyb, 0, 0))
+        put_grad(VAL, dot(hbuf[...], dqkv[:, vcols], 0, 0))
+        for u in (OUT, VAL):
+            stage_pair(u, step)
+
+        @pl.when(l > 0)
+        def _():
+            dhacc[...] = dot(dqkv[:, vcols], wcat[l, :, vcols], 1, 1)
+
+        pl.when(step >= 2)(older)
         finish_gather(dlog)
 
         for p in range(PAIRS):
@@ -257,21 +619,54 @@
 
         @pl.when(l > 0)
         def _():
-            dh = dhacc[...] + dot(dqkv[:, qk], wq[l, :, qk], 1, 1)
-            dn = dh.astype(BF).astype(F32) * gain_ref[l]
+            dh = dhacc[...] + dot(dqkv[:, qk], wcat[l, :, qk], 1, 1)
+            dn = dh.astype(BF).astype(F32) * gains[l]
             first = jnp.mean(dn, axis=-1, keepdims=True)
             second = jnp.mean(dn * normal, axis=-1, keepdims=True)
             dyf[...] = dyf[...] + rstd * (dn - first - normal * second)
 
-        for n in range(2):
-            cols = pl.ds(WIDTH * n, WIDTH)
-            gq[:, cols] = dot(hbuf[...], dqkv[:, cols], 0, 0).astype(BF)
-        pltpu.make_async_copy(gq, gq_hbm.at[l], g_sem.at[0]).start()
         return carry
 
     lax.fori_loop(0, LAYERS, backward, 0)
-    pltpu.make_async_copy(gq, gq_hbm.at[0], g_sem.at[0]).wait()
-    pltpu.make_async_copy(go, go_hbm.at[0], g_sem.at[1]).wait()
+
+    for work in reduce_window(LAYERS) + gather_window(LAYERS):
+        work()
+    reduce_window(LAYERS + 1)[0]()
+    gather_window(LAYERS + 1)[1]()
+
+    for u in range(4):
+
+        @pl.when(sec != 0)
+        def _():
+            x_copy(u, LAYERS - 1).wait_send()
+
+        total = fin[u]
+        for slot in range(LAYERS - 1):
+            pltpu.make_async_remote_copy(
+                src_ref=xout.at[u],
+                dst_ref=xin.at[u, slot],
+                send_sem=x_send.at[u],
+                recv_sem=x_recv.at[u, slot],
+                device_id=(lax.rem(sec + 1, LAYERS), me),
+                device_id_type=MESH,
+            ).wait_recv()
+            total = total + xin[u, slot].astype(F32)
+        if u == OUT:
+            go_ref[0] = total
+        else:
+            gq_ref[0, :, pl.ds(WIDTH * {VAL: 2, QRY: 0, KEY: 1}[u], WIDTH)] = total
+
+    drain(0, True)
+    for l in range(1, LAYERS):
+        drain(l)
+
+    @pl.when(sec == 0)
+    def _():
+        for t in range(1, LAYERS):
+            tab_copy(t).wait_send()
+
+    for d in range(1, LAYERS):
+        gain_copy(d).wait_send()
 
 
 def local(tokens, embed, ln_gain, w_qkv, w_out, out_grad):
@@ -284,22 +679,22 @@
     scale = HEAD_DIM ** (-0.5) / (rows_here * n_row) ** 0.5
     tok = lax.dynamic_index_in_dim(tokens, section, 0, keepdims=False).reshape(npos, 1)
     emb = jnp.pad(embed, ((0, -vocab % 16), (0, 0)))
-    gains = lax.all_gather(ln_gain, "section", axis=0, tiled=False)
-    wqkv = lax.all_gather(w_qkv, "section", axis=0, tiled=True)
-    wout = lax.all_gather(w_out, "section", axis=0, tiled=True)
     flat = HEADS * seq
+    own_rows = width // n_row
     vm, anyspace = pl.BlockSpec(memory_space=pltpu.VMEM), pl.BlockSpec(memory_space=pl.ANY)
-    gq, go = pl.pallas_call(
+    dma = pltpu.SemaphoreType.DMA
+    grad_qkv, grad_out = pl.pallas_call(
         functools.partial(kernel, n_row, scale),
         out_shape=(
-            jax.ShapeDtypeStruct((LAYERS, width, 3 * width), BF),
-            jax.ShapeDtypeStruct((LAYERS, width, width), BF),
+            jax.ShapeDtypeStruct((1, own_rows, 3 * width), F32),
+            jax.ShapeDtypeStruct((1, own_rows, width), F32),
         ),
         in_specs=[vm, vm, vm, anyspace, anyspace, anyspace],
-        out_specs=(anyspace, anyspace),
+        out_specs=(vm, vm),
         scratch_shapes=[
-            pltpu.VMEM((LAYERS, width, 3 * width), BF),
-            pltpu.VMEM((LAYERS, width, width), BF),
+            pltpu.VMEM((LAYERS, width, 4 * width), BF),
+            pltpu.VMEM((LAYERS, 1, width), F32),
+            pltpu.VMEM((emb.shape[0], 3 * width), BF),
             pltpu.VMEM((LAYERS, npos, width), F32),
             pltpu.VMEM((LAYERS, npos, 3 * width), BF),
             pltpu.VMEM((LAYERS, flat, seq), BF),
@@ -313,28 +708,41 @@
             pltpu.VMEM((npos, 3 * width), BF),
             pltpu.VMEM((npos, width), BF),
             pltpu.VMEM((npos, width), F32),
-            pltpu.VMEM((width, 3 * width), BF),
-            pltpu.VMEM((width, width), BF),
-            pltpu.SemaphoreType.DMA((n_row,)),
-            pltpu.SemaphoreType.DMA((n_row,)),
-            pltpu.SemaphoreType.DMA((n_row,)),
-            pltpu.SemaphoreType.DMA((n_row,)),
-            pltpu.SemaphoreType.DMA((2, LAYERS)),
-            pltpu.SemaphoreType.DMA,
-            pltpu.SemaphoreType.DMA((2,)),
+            pltpu.VMEM((4, 2, SIDE, SIDE, own_rows, width), BF),
+            pltpu.VMEM((2, 4, SIDE, SIDE, own_rows, width), BF),
+            pltpu.VMEM((2, 4, SIDE - 1, SIDE, own_rows, width), BF),
+            pltpu.VMEM((2, 4, SIDE, own_rows, width), BF),
+            pltpu.VMEM((2, 4, SIDE - 1, own_rows, width), BF),
+            pltpu.VMEM((4, own_rows, width), BF),
+            pltpu.VMEM((4, LAYERS - 1, own_rows, width), BF),
+            pltpu.VMEM((4, own_rows, width), F32),
+            dma((n_row,)),
+            dma((n_row,)),
+            dma((n_row,)),
+            dma((n_row,)),
+            dma((2,)),
+            dma,
+            dma((LAYERS,)),
+            dma,
+            dma((LAYERS,)),
+            dma((LAYERS,)),
+            dma((LAYERS, 2, CHUNKS)),
+            dma((LAYERS, 2, CHUNKS)),
+            dma((LAYERS, 2, CHUNKS)),
+            dma((LAYERS, 2, CHUNKS)),
+            dma((4,)),
+            dma((2, 4)),
+            dma((4, SIDE - 1)),
+            dma((2, 4, SIDE - 1)),
+            dma((4, SIDE - 1)),
+            dma((2, 4, SIDE - 1)),
+            dma((4,)),
+            dma((4, LAYERS - 1)),
         ],
         compiler_params=pltpu.CompilerParams(
-            collective_id=0, has_side_effects=True, vmem_limit_bytes=64 * 1024 * 1024 - 1024 * 1024
+            collective_id=0, has_side_effects=True, vmem_limit_bytes=67043328
         ),
-    )(tok, emb, gains, wqkv, wout, out_grad.reshape(micro, npos, width))
-
-    def reduced(g):
-        g = lax.psum_scatter(g, "section", scatter_dimension=0, tiled=True)
-        return lax.psum_scatter(g.astype(F32), "row", scatter_dimension=1, tiled=True)
-
-    grad_qkv = reduced(gq)
-    grad_out = reduced(go)
-    own_rows = width // n_row
+    )(tok, emb, ln_gain, w_qkv, w_out, out_grad.reshape(micro, npos, width))
     w_own = lax.dynamic_slice_in_dim(w_qkv[0], row * own_rows, own_rows, 0).astype(F32)
     gain_own = lax.dynamic_slice_in_dim(ln_gain[0], row * own_rows, own_rows, 0)
     grad_gain = (jnp.sum(w_own * grad_qkv[0], axis=-1) / gain_own)[None]

time: 708 us -> 328 us (0.46)
  waiting for transfers between devices: 521 us -> 0 us
  Pallas kernels: 148 us -> 318 us
  between operations: 14.2 us -> 0.65 us
  blocking collectives: 12.7 us -> 0 us
  other arithmetic: 10.1 us -> 2.42 us
    reduce_scatter x4 -> x0, waiting for transfers between devices: 344 us -> none  [the longest x2 174 us: reduced(): g = lax.psum_scatter(g, 'section', scatter_dimension=0, tiled=True)]
    all_gather x2 -> x0, waiting for transfers between devices: 176 us -> none  [the longest x1 134 us: local(): wqkv = lax.all_gather(w_qkv, 'section', axis=0, tiled=True)]
    pallas_call x1, Pallas kernels: 148 us -> 318 us  [local(): pl.pallas_call(functools.partial(kernel, n_row, scale), out_shape=(jax.Sh...]
    all_gather x1 -> x0, blocking collectives: 12.7 us -> none  [local(): gains = lax.all_gather(ln_gain, 'section', axis=0, tiled=False)]
    convert_element_type x2 -> x0, other arithmetic: 8.33 us -> none  [reduced(): g.astype(F32)]
  transfers between devices with their start and end apart: 6 -> 0, of which waited for: 6 -> 0; matrix products, arithmetic and copies ran while one was open for 2% -> 0% of each run, Pallas kernels for 0% -> 0%
where the time goes in v2:
time: 328 us; the launch traced here: 327 us
  Pallas kernels  318 us (97%)
  local copies, waits for them, and re-layouts  6.11 us (2%)
    pallas_call x1, Pallas kernels, local(): pl.pallas_call(functools.partial(kernel, n_row, scale), out_shape=(jax.Sh...  318 us

profile of v2, /device:TPU:0, one launch (start us, length us, event | category | flops | bytes accessed | tf_op | source)
XLA Modules:
  0.0 327.2 jit_solution(13420758941881443460)
XLA Ops:
  0.6 0.7 constant_dynamic-slice_fusion.1
  1.3 1.5 pad.4.emb_ref
  2.8 0.8 copy.9.tok_ref
  3.6 318.1 %shard_map.85 = (f32[1,24,2304]{2,1,0:T(8,128)}, f32[1,24,768]{2,1,0:T(8,128)}) custom-call(s32[256,1]{1,0:T(8,128)} %copy.9.tok_ref, bf16[48,768]{1,0:T(8,128)(2,1)} %pad.4.emb_ref, f32[1,768]{1,0:T(1,128)} %gain_ref.1, bf16[1,768,2304]{2,1,0:T(8,128)(2,1)} %wqkv_hbm.1, bf16[1,768,768]{2,1,0:T(8,128)(2,1)} %wout_hbm.1, bf16[4,256,768]{2,1,0:T(8,128)(2,1)} %bitcast.4), custom_call_target="tpu_custom_call" | custom-call | tf_op jit(solution)/shard_map/pallas_call | solution.py:686
  321.7 1.1 multiply_reduce_fusion
  322.8 1.3 fusion
  324.1 1.6 copy.12
  325.7 1.5 copy.13

commit v3 on v2

--- a/solution.py
+++ b/solution.py
@@ -18,6 +18,7 @@
 CHUNKS = 6
 CHUNKS_FIRST = 2
 QUARTER = WIDTH // 4
+HALF = WIDTH // 2
 MESH = pl.DeviceIdType.MESH
 BF = jnp.bfloat16
 F32 = jnp.float32
@@ -47,6 +48,7 @@
     go_ref,
     wcat,
     gains,
+    embp,
     tab,
     xs,
     qkv,
@@ -79,6 +81,14 @@
     tab_recv,
     gain_send,
     gain_recv,
+    deal_send,
+    deal_recv,
+    s1_send,
+    s1_recv,
+    s2_send,
+    s2_recv,
+    join_send,
+    join_recv,
     ring_send,
     ring_recv,
     twin_send,
@@ -104,11 +114,15 @@
     def row_at(z, y):
         return (z * SIDE + y) * 2 + core
 
+    def weight(l, first, count):
+        block = wcat[l, :, :, :, pl.ds(first, count)]
+        return block.reshape(WIDTH, count)
+
     local_qkv = pltpu.make_async_copy(
-        wqkv_hbm.at[0], wcat.at[sec, :, pl.ds(0, 3 * WIDTH)], w_sem.at[0]
+        wqkv_hbm, wcat.at[sec, :, :, :, pl.ds(0, 3 * WIDTH)], w_sem.at[0]
     )
     local_out = pltpu.make_async_copy(
-        wout_hbm.at[0], wcat.at[sec, :, pl.ds(3 * WIDTH, WIDTH)], w_sem.at[1]
+        wout_hbm, wcat.at[sec, :, :, :, pl.ds(3 * WIDTH, WIDTH)], w_sem.at[1]
     )
     local_qkv.start()
     local_out.start()
@@ -132,31 +146,47 @@
     high = (lane >= HEAD_DIM).astype(F32).astype(BF)
 
     gains[sec] = gain_ref[...]
-    vocab = emb_ref.shape[0]
-    ids = lax.broadcasted_iota(jnp.int32, (tok_ref.shape[0], vocab), 1)
-    picks = (tok_ref[...] == ids).astype(F32).astype(BF)
-    xs[0] = dot(picks, emb_ref[...], 1, 0)
+    padded = embp.shape[0]
+    embp[...] = jnp.zeros_like(embp)
+    embp[pl.ds(0, emb_ref.shape[0]), :] = emb_ref[...]
+    ids = lax.broadcasted_iota(jnp.int32, (padded, SEQ), 0)
+    tok = tok_ref[sec]
+    picks = jnp.concatenate([(tok[r : r + 1] == ids) for r in range(2)], axis=1)
+    picks = picks.astype(F32).astype(BF)
+    xs[0] = dot(picks, embp[...], 0, 0)
 
     local_qkv.wait()
 
     @pl.when(sec == 0)
     def _():
-        normal, _ = norm_parts(emb_ref[...].astype(F32))
+        normal, _ = norm_parts(embp[...].astype(F32))
         h = (normal * gain_ref[...]).astype(BF)
         for n in range(3):
-            cols = pl.ds(WIDTH * n, WIDTH)
-            tab[:, cols] = dot(h, wcat[0, :, cols], 1, 0).astype(BF)
+            made = dot(h, weight(0, WIDTH * n, WIDTH), 1, 0).astype(BF)
+            for half in range(2):
+                cols = pl.ds(HALF * n, HALF)
+                tab[half, :, cols] = made[:, HALF * half : HALF * (half + 1)]
 
     local_out.wait()
     pl.semaphore_wait(barrier, n_row - 1 + LAYERS - 1)
 
     def tab_copy(t):
         return pltpu.make_async_remote_copy(
-            src_ref=tab,
-            dst_ref=tab,
+            src_ref=tab.at[core],
+            dst_ref=tab.at[core],
             send_sem=tab_send.at[t],
-            recv_sem=tab_recv,
+            recv_sem=tab_recv.at[0],
             device_id=(t, me),
+            device_id_type=MESH,
+        )
+
+    def tab_twin(who):
+        return pltpu.make_async_remote_copy(
+            src_ref=tab.at[who],
+            dst_ref=tab.at[who],
+            send_sem=tab_send.at[0],
+            recv_sem=tab_recv.at[1],
+            device_id=(sec, partner),
             device_id_type=MESH,
         )
 
@@ -179,12 +209,10 @@
         gain_copy(d).start()
 
     def flow(l, d, k, who, first):
-        rows = QUARTER // (CHUNKS_FIRST if first else CHUNKS)
-        start = who * (2 * QUARTER) + d * QUARTER + k * rows
-        span = pl.ds(pl.multiple_of(start, 16), rows)
+        block = who * 2 + d
         if first:
-            return wcat.at[0, span, pl.ds(3 * WIDTH, WIDTH)]
-        return wcat.at[l, span]
+            return wcat.at[0, block, k, :, pl.ds(3 * WIDTH, WIDTH)]
+        return wcat.at[l, block, k // 3, pl.ds(pl.multiple_of(lax.rem(k, 3) * 32, 16), 32)]
 
     def place(l, d):
         return lax.rem(sec - l + LAYERS, LAYERS) if d == 0 else lax.rem(l - sec + LAYERS, LAYERS)
@@ -264,6 +292,98 @@
             return carry
 
         lax.fori_loop(0, chunks, one, 0)
+
+    block_cols = pl.ds(pl.multiple_of((core * SIDE + yc) * HALF, 128), HALF)
+
+    def side_cols(who):
+        return pl.ds(pl.multiple_of(who * (2 * WIDTH), 128), 2 * WIDTH)
+
+    def deal_copy(d):
+        ref = wcat.at[1, zc, :, :, block_cols]
+        return pltpu.make_async_remote_copy(
+            src_ref=ref,
+            dst_ref=ref,
+            send_sem=deal_send.at[d],
+            recv_sem=deal_recv,
+            device_id=(lax.rem(1 + d, LAYERS), me),
+            device_id_type=MESH,
+        )
+
+    def line_copy(stage, half, d):
+        along_y = (stage + half) % 2 == 0
+        y = lax.rem(yc + d, SIDE) if along_y else yc
+        z = zc if along_y else lax.rem(zc + d, SIDE)
+        if stage == 0:
+            ref = wcat.at[1, zc, half, :, block_cols]
+        elif along_y:
+            ref = wcat.at[1, :, half, :, block_cols]
+        else:
+            ref = wcat.at[1, zc, half, :, side_cols(core)]
+        send, take = (s1_send, s1_recv) if stage == 0 else (s2_send, s2_recv)
+        return pltpu.make_async_remote_copy(
+            src_ref=ref,
+            dst_ref=ref,
+            send_sem=send.at[half, d - 1],
+            recv_sem=take.at[half, d - 1],
+            device_id=(sec, row_at(z, y)),
+            device_id_type=MESH,
+        )
+
+    def join_copy(half, who):
+        ref = wcat.at[1, :, half, :, side_cols(who)]
+        return pltpu.make_async_remote_copy(
+            src_ref=ref,
+            dst_ref=ref,
+            send_sem=join_send.at[half],
+            recv_sem=join_recv.at[half],
+            device_id=(sec, partner),
+            device_id_type=MESH,
+        )
+
+    def plane_one():
+        @pl.when(sec != 1)
+        def _():
+            deal_copy(0).wait_recv()
+            for half in range(2):
+                for d in range(1, SIDE):
+                    line_copy(0, half, d).start()
+
+    def plane_two():
+        @pl.when(sec != 1)
+        def _():
+            for half in range(2):
+                for d in range(1, SIDE):
+                    line_copy(0, half, d).wait_recv()
+                for d in range(1, SIDE):
+                    line_copy(1, half, d).start()
+
+    def plane_three():
+        @pl.when(sec != 1)
+        def _():
+            for half in range(2):
+                for d in range(1, SIDE):
+                    line_copy(1, half, d).wait_recv()
+                join_copy(half, core).start()
+
+    def plane_settle():
+        @pl.when(sec != 1)
+        def _():
+            for half in range(2):
+                join_copy(half, 1 - core).wait_recv()
+
+    def plane_drain():
+        @pl.when(sec != 1)
+        def _():
+            for half in range(2):
+                for d in range(1, SIDE):
+                    line_copy(0, half, d).wait_send()
+                    line_copy(1, half, d).wait_send()
+                join_copy(half, core).wait_send()
+
+        @pl.when(sec == 1)
+        def _():
+            for d in range(1, LAYERS):
+                deal_copy(d).wait_send()
 
     def rows_of(k):
         return pl.ds(pl.multiple_of(k * piece, 16), piece)
@@ -460,8 +580,13 @@
             xout[u] = total.astype(BF)
             x_copy(u, t).start()
 
+    @pl.when(sec == 1)
+    def _():
+        for d in range(1, LAYERS):
+            deal_copy(d).start()
+
     launch_flow(0, True)
-    launch_flow(1)
+    launch_flow(2)
 
     def forward(l, carry):
         here = qkv.at[l]
@@ -471,38 +596,46 @@
             @pl.when(sec > 0)
             def _():
                 tab_copy(0).wait_recv()
+                tab_twin(core).start()
+                tab_twin(1 - core).wait_recv()
 
             for d in range(1, LAYERS):
                 gain_copy(d).wait_recv()
             for n in range(3):
-                cols = pl.ds(WIDTH * n, WIDTH)
-                here[:, cols] = dot(picks, tab[:, cols], 1, 0).astype(BF)
+                for half in range(2):
+                    made = dot(picks, tab[half, :, pl.ds(HALF * n, HALF)], 0, 0)
+                    here[:, pl.ds(WIDTH * n + HALF * half, HALF)] = made.astype(BF)
 
         @pl.when(l > 0)
         def _():
-            settle(l)
+            pl.when(l == 1)(plane_settle)
+            pl.when(l > 1)(lambda: settle(l))
             normal, _ = norm_parts(xs[l])
             h = (normal * gains[l]).astype(BF)
             for n in range(3):
                 cols = pl.ds(WIDTH * n, WIDTH)
-                here[:, cols] = dot(h, wcat[l, :, cols], 1, 0).astype(BF)
+                here[:, cols] = dot(h, weight(l, WIDTH * n, WIDTH), 1, 0).astype(BF)
 
         pair_scores(lambda p: halves(here, 0, p), lambda p: halves(here, WIDTH, p), scale)
         start_reduce()
 
         @pl.when(l == 0)
         def _():
+            plane_one()
             for slot in range(1, CHUNKS_FIRST + 3):
                 pump(0, slot, True)
-
-        @pl.when((l > 0) & (l < LAYERS - 1))
-        def _():
-            launch_flow(l + 1)
-
-        @pl.when(l < LAYERS - 1)
-        def _():
-            for slot in range(1, 5):
-                pump(l + 1, slot)
+            for slot in range(1, 4):
+                pump(2, slot)
+
+        @pl.when(l == 1)
+        def _():
+            for slot in range(7, CHUNKS + 3):
+                pump(2, slot)
+
+        @pl.when(l == 2)
+        def _():
+            for slot in range(4, 7):
+                pump(3, slot)
 
         logits = finish_reduce()
         shifted = jnp.exp(logits - jnp.max(logits, axis=-1, keepdims=True))
@@ -511,10 +644,22 @@
         probs_l[rows_of(me), :] = own.astype(BF)
         start_gather(probs_l)
 
-        @pl.when(l < LAYERS - 1)
-        def _():
-            for slot in range(5, CHUNKS + 3):
-                pump(l + 1, slot)
+        @pl.when(l == 0)
+        def _():
+            plane_two()
+            for slot in range(4, 7):
+                pump(2, slot)
+            launch_flow(3)
+
+        @pl.when(l == 1)
+        def _():
+            for slot in range(1, 4):
+                pump(3, slot)
+
+        @pl.when(l == 2)
+        def _():
+            for slot in range(7, CHUNKS + 3):
+                pump(3, slot)
 
         finish_gather(probs_l)
         mixed_l = mixed.at[l]
@@ -524,11 +669,12 @@
 
         @pl.when(l == 0)
         def _():
+            plane_three()
             settle(0, True)
 
         @pl.when(l < LAYERS - 1)
         def _():
-            xs[l + 1] = xs[l] + dot(mixed_l[...], wcat[l, :, pl.ds(3 * WIDTH, WIDTH)], 1, 0)
+            xs[l + 1] = xs[l] + dot(mixed_l[...], weight(l, 3 * WIDTH, WIDTH), 1, 0)
 
         return carry
 
@@ -575,7 +721,7 @@
         here = qkv.at[l]
         probs_l = probs.at[l]
         dyb = dyf[...].astype(BF)
-        dmix[...] = dot(dyb, wcat[l, :, pl.ds(3 * WIDTH, WIDTH)], 1, 1).astype(BF)
+        dmix[...] = dot(dyb, weight(l, 3 * WIDTH, WIDTH), 1, 1).astype(BF)
         pair_scores(lambda p: halves(dmix, 0, p), lambda p: halves(here, 2 * WIDTH, p), None)
         start_reduce()
 
@@ -604,7 +750,7 @@
 
         @pl.when(l > 0)
         def _():
-            dhacc[...] = dot(dqkv[:, vcols], wcat[l, :, vcols], 1, 1)
+            dhacc[...] = dot(dqkv[:, vcols], weight(l, 2 * WIDTH, WIDTH), 1, 1)
 
         pl.when(step >= 2)(older)
         finish_gather(dlog)
@@ -619,7 +765,7 @@
 
         @pl.when(l > 0)
         def _():
-            dh = dhacc[...] + dot(dqkv[:, qk], wcat[l, :, qk], 1, 1)
+            dh = dhacc[...] + dot(dqkv[:, qk], weight(l, 0, 2 * WIDTH), 1, 1)
             dn = dh.astype(BF).astype(F32) * gains[l]
             first = jnp.mean(dn, axis=-1, keepdims=True)
             second = jnp.mean(dn * normal, axis=-1, keepdims=True)
@@ -657,28 +803,31 @@
             gq_ref[0, :, pl.ds(WIDTH * {VAL: 2, QRY: 0, KEY: 1}[u], WIDTH)] = total
 
     drain(0, True)
-    for l in range(1, LAYERS):
+    for l in range(2, LAYERS):
         drain(l)
+    plane_drain()
 
     @pl.when(sec == 0)
     def _():
         for t in range(1, LAYERS):
             tab_copy(t).wait_send()
 
+    @pl.when(sec > 0)
+    def _():
+        tab_twin(core).wait_send()
+
     for d in range(1, LAYERS):
         gain_copy(d).wait_send()
 
 
 def local(tokens, embed, ln_gain, w_qkv, w_out, out_grad):
     n_row = lax.axis_size("row")
-    section = lax.axis_index("section")
     row = lax.axis_index("row")
     micro, rows_here, seq = tokens.shape
     vocab, width = embed.shape
     npos = rows_here * seq
     scale = HEAD_DIM ** (-0.5) / (rows_here * n_row) ** 0.5
-    tok = lax.dynamic_index_in_dim(tokens, section, 0, keepdims=False).reshape(npos, 1)
-    emb = jnp.pad(embed, ((0, -vocab % 16), (0, 0)))
+    padded = vocab + -vocab % 16
     flat = HEADS * seq
     own_rows = width // n_row
     vm, anyspace = pl.BlockSpec(memory_space=pltpu.VMEM), pl.BlockSpec(memory_space=pl.ANY)
@@ -692,9 +841,10 @@
         in_specs=[vm, vm, vm, anyspace, anyspace, anyspace],
         out_specs=(vm, vm),
         scratch_shapes=[
-            pltpu.VMEM((LAYERS, width, 4 * width), BF),
+            pltpu.VMEM((LAYERS, SIDE, 2, width // 8, 4 * width), BF),
             pltpu.VMEM((LAYERS, 1, width), F32),
-            pltpu.VMEM((emb.shape[0], 3 * width), BF),
+            pltpu.VMEM((padded, width), BF),
+            pltpu.VMEM((2, padded, 3 * width // 2), BF),
             pltpu.VMEM((LAYERS, npos, width), F32),
             pltpu.VMEM((LAYERS, npos, 3 * width), BF),
             pltpu.VMEM((LAYERS, flat, seq), BF),
@@ -723,9 +873,17 @@
             dma((2,)),
             dma,
             dma((LAYERS,)),
-            dma,
+            dma((2,)),
             dma((LAYERS,)),
             dma((LAYERS,)),
+            dma((LAYERS,)),
+            dma,
+            dma((2, SIDE - 1)),
+            dma((2, SIDE - 1)),
+            dma((2, SIDE - 1)),
+            dma((2, SIDE - 1)),
+            dma((2,)),
+            dma((2,)),
             dma((LAYERS, 2, CHUNKS)),
             dma((LAYERS, 2, CHUNKS)),
             dma((LAYERS, 2, CHUNKS)),
@@ -742,7 +900,14 @@
         compiler_params=pltpu.CompilerParams(
             collective_id=0, has_side_effects=True, vmem_limit_bytes=67043328
         ),
-    )(tok, emb, ln_gain, w_qkv, w_out, out_grad.reshape(micro, npos, width))
+    )(
+        tokens,
+        embed,
+        ln_gain,
+        w_qkv.reshape(SIDE, 2, width // 8, 3 * width),
+        w_out.reshape(SIDE, 2, width // 8, width),
+        out_grad.reshape(micro, npos, width),
+    )
     w_own = lax.dynamic_slice_in_dim(w_qkv[0], row * own_rows, own_rows, 0).astype(F32)
     gain_own = lax.dynamic_slice_in_dim(ln_gain[0], row * own_rows, own_rows, 0)
     grad_gain = (jnp.sum(w_own * grad_qkv[0], axis=-1) / gain_own)[None]

time: 328 us -> 272 us (0.83)
  Pallas kernels: 318 us -> 266 us
    pallas_call x1, Pallas kernels: 318 us -> 266 us  [local(): pl.pallas_call(functools.partial(kernel, n_row, scale), out_shape=(jax.Sh...]
where the time goes in v3:
time: 272 us
  Pallas kernels  266 us (98%)
  local copies, waits for them, and re-layouts  3.15 us (1%)
    pallas_call x1, Pallas kernels, local(): pl.pallas_call(functools.partial(kernel, n_row, scale), out_shape=(jax.Sh...  266 us

profile of v3, /device:TPU:0, one launch (start us, length us, event | category | flops | bytes accessed | tf_op | source)
XLA Modules:
  0.0 271.8 jit_solution(11380837843382781723)
XLA Ops:
  0.6 265.6 %shard_map.85 = (f32[1,24,2304]{2,1,0:T(8,128)}, f32[1,24,768]{2,1,0:T(8,128)}) custom-call(s32[4,2,128]{2,1,0:T(2,128)} %tok_ref.1, bf16[33,768]{1,0:T(8,128)(2,1)} %emb_ref.1, f32[1,768]{1,0:T(1,128)} %gain_ref.1, bf16[4,2,96,2304]{3,2,1,0:T(8,128)(2,1)} %bitcast.5, bf16[4,2,96,768]{3,2,1,0:T(8,128)(2,1)} %bitcast.7, bf16[4,256,768]{2,1,0:T(8,128)(2,1)} %bitcast.6), custom_call_target="tpu_custom_call" | custom-call | tf_op jit(solution)/shard_map/pallas_call | solution.py:835
  266.3 1.1 multiply_reduce_fusion
  267.4 1.3 bitcast_divide_fusion
  268.7 1.6 copy.11
  270.3 1.5 copy.12

commit v4 on v3

--- a/solution.py
+++ b/solution.py
@@ -15,9 +15,8 @@
 SEQ = 128
 SIDE = 4
 OUT, VAL, QRY, KEY = 0, 1, 2, 3
-CHUNKS = 6
-CHUNKS_FIRST = 2
-QUARTER = WIDTH // 4
+CHUNKS = 3
+CHUNK = 4 * WIDTH // CHUNKS
 HALF = WIDTH // 2
 MESH = pl.DeviceIdType.MESH
 BF = jnp.bfloat16
@@ -55,6 +54,8 @@
     probs,
     mixed,
     part,
+    other,
+    both,
     recv,
     dlog,
     dyf,
@@ -71,10 +72,13 @@
     xout,
     xin,
     fin,
+    level_sem,
     rs_send,
     rs_recv,
     ag_send,
     ag_recv,
+    hand_send,
+    hand_recv,
     w_sem,
     og_sem,
     tab_send,
@@ -93,6 +97,8 @@
     ring_recv,
     twin_send,
     twin_recv,
+    first_send,
+    first_recv,
     pair_send,
     pair_recv,
     c1_send,
@@ -105,6 +111,7 @@
     sec = lax.axis_index("section")
     me = lax.axis_index("row")
     piece = part.shape[0] // n_row
+    n_chip = n_row // 2
     core = lax.rem(me, 2)
     partner = me + 1 - 2 * core
     chip = me // 2
@@ -131,11 +138,12 @@
     barrier = pltpu.get_barrier_semaphore()
 
     def greet(d, carry):
-        peer = lax.rem(me + d, n_row)
+        peer = 2 * lax.rem(chip + d, n_chip) + core
         pl.semaphore_signal(barrier, inc=1, device_id=(sec, peer), device_id_type=MESH)
         return carry
 
-    lax.fori_loop(1, n_row, greet, 0)
+    lax.fori_loop(1, n_chip, greet, 0)
+    pl.semaphore_signal(barrier, inc=1, device_id=(sec, partner), device_id_type=MESH)
     for d in range(1, LAYERS):
         pl.semaphore_signal(
             barrier, inc=1, device_id=(lax.rem(sec + d, LAYERS), me), device_id_type=MESH
@@ -168,7 +176,7 @@
                 tab[half, :, cols] = made[:, HALF * half : HALF * (half + 1)]
 
     local_out.wait()
-    pl.semaphore_wait(barrier, n_row - 1 + LAYERS - 1)
+    pl.semaphore_wait(barrier, n_chip + LAYERS - 1)
 
     def tab_copy(t):
         return pltpu.make_async_remote_copy(
@@ -208,185 +216,204 @@
     for d in range(1, LAYERS):
         gain_copy(d).start()
 
-    def flow(l, d, k, who, first):
-        block = who * 2 + d
-        if first:
-            return wcat.at[0, block, k, :, pl.ds(3 * WIDTH, WIDTH)]
-        return wcat.at[l, block, k // 3, pl.ds(pl.multiple_of(lax.rem(k, 3) * 32, 16), 32)]
-
-    def place(l, d):
-        return lax.rem(sec - l + LAYERS, LAYERS) if d == 0 else lax.rem(l - sec + LAYERS, LAYERS)
-
-    def ring_copy(l, d, k, first):
+    RING = LAYERS - 1
+
+    def flow(d, k, who):
+        cols = pl.ds(pl.multiple_of(k * CHUNK, 128), CHUNK)
+        return wcat.at[RING, who * 2 + d, :, :, cols]
+
+    def place(d):
+        return lax.rem(sec - RING + LAYERS, LAYERS) if d == 0 else lax.rem(RING - sec, LAYERS)
+
+    def ring_copy(d, k):
         step = 1 if d == 0 else LAYERS - 1
-        ref = flow(l, d, k, core, first)
+        ref = flow(d, k, core)
         return pltpu.make_async_remote_copy(
             src_ref=ref,
             dst_ref=ref,
-            send_sem=ring_send.at[l, d, k],
-            recv_sem=ring_recv.at[l, d, k],
+            send_sem=ring_send.at[d, k],
+            recv_sem=ring_recv.at[d, k],
             device_id=(lax.rem(sec + step, LAYERS), me),
             device_id_type=MESH,
         )
 
-    def twin_copy(l, d, k, who, first):
-        ref = flow(l, d, k, who, first)
+    def twin_copy(d, k, who):
+        ref = flow(d, k, who)
         return pltpu.make_async_remote_copy(
             src_ref=ref,
             dst_ref=ref,
-            send_sem=twin_send.at[l, d, k],
-            recv_sem=twin_recv.at[l, d, k],
+            send_sem=twin_send.at[d, k],
+            recv_sem=twin_recv.at[d, k],
             device_id=(sec, partner),
             device_id_type=MESH,
         )
 
-    def launch_flow(l, first=False):
-        chunks = CHUNKS_FIRST if first else CHUNKS
-
-        @pl.when(sec == l)
-        def _():
-            for k in range(chunks):
+    def launch_flow():
+        @pl.when(sec == RING)
+        def _():
+            for k in range(CHUNKS):
                 for d in range(2):
-                    ring_copy(l, d, k, first).start()
-
-    def pump(l, slot, first=False):
-        chunks = CHUNKS_FIRST if first else CHUNKS
+                    ring_copy(d, k).start()
+
+    def pump(slot):
         for d in range(2):
-            at = place(l, d)
+            at = place(d)
             k = slot - at
 
-            @pl.when((at > 0) & (k >= 0) & (k < chunks))
+            @pl.when((at > 0) & (k >= 0) & (k < CHUNKS))
             def _():
-                ring_copy(l, d, k, first).wait_recv()
+                ring_copy(d, k).wait_recv()
 
                 @pl.when(at < LAYERS - 1)
                 def _():
-                    ring_copy(l, d, k, first).start()
-
-                twin_copy(l, d, k, core, first).start()
-
-    def settle(l, first=False):
-        chunks = CHUNKS_FIRST if first else CHUNKS
-
-        @pl.when(sec != l)
-        def _():
-            for k in range(chunks):
+                    ring_copy(d, k).start()
+
+                twin_copy(d, k, core).start()
+
+    def settle():
+        @pl.when(sec != RING)
+        def _():
+            for k in range(CHUNKS):
                 for d in range(2):
-                    twin_copy(l, d, k, 1 - core, first).wait_recv()
-
-    def drain(l, first=False):
-        chunks = CHUNKS_FIRST if first else CHUNKS
-
+                    twin_copy(d, k, 1 - core).wait_recv()
+
+    def drain():
         def one(k, carry):
             for d in range(2):
-                at = place(l, d)
+                at = place(d)
 
                 @pl.when(at < LAYERS - 1)
                 def _():
-                    ring_copy(l, d, k, first).wait_send()
+                    ring_copy(d, k).wait_send()
 
                 @pl.when(at > 0)
                 def _():
-                    twin_copy(l, d, k, core, first).wait_send()
+                    twin_copy(d, k, core).wait_send()
 
             return carry
 
-        lax.fori_loop(0, chunks, one, 0)
+        lax.fori_loop(0, CHUNKS, one, 0)
+
+    def first_ref(who):
+        return wcat.at[0, pl.ds(2 * who, 2), :, :, pl.ds(3 * WIDTH, WIDTH)]
+
+    def first_copy(t):
+        return pltpu.make_async_remote_copy(
+            src_ref=first_ref(core),
+            dst_ref=first_ref(core),
+            send_sem=first_send.at[t],
+            recv_sem=first_recv.at[0],
+            device_id=(t, me),
+            device_id_type=MESH,
+        )
+
+    def first_twin(who):
+        return pltpu.make_async_remote_copy(
+            src_ref=first_ref(who),
+            dst_ref=first_ref(who),
+            send_sem=first_send.at[0],
+            recv_sem=first_recv.at[1],
+            device_id=(sec, partner),
+            device_id_type=MESH,
+        )
 
     block_cols = pl.ds(pl.multiple_of((core * SIDE + yc) * HALF, 128), HALF)
 
     def side_cols(who):
         return pl.ds(pl.multiple_of(who * (2 * WIDTH), 128), 2 * WIDTH)
 
-    def deal_copy(d):
-        ref = wcat.at[1, zc, :, :, block_cols]
+    def deal_copy(w, d):
+        ref = wcat.at[w, zc, :, :, block_cols]
         return pltpu.make_async_remote_copy(
             src_ref=ref,
             dst_ref=ref,
-            send_sem=deal_send.at[d],
-            recv_sem=deal_recv,
-            device_id=(lax.rem(1 + d, LAYERS), me),
-            device_id_type=MESH,
-        )
-
-    def line_copy(stage, half, d):
+            send_sem=deal_send.at[w - 1, d],
+            recv_sem=deal_recv.at[w - 1],
+            device_id=((w + d) % LAYERS, me),
+            device_id_type=MESH,
+        )
+
+    def line_copy(w, stage, half, d):
         along_y = (stage + half) % 2 == 0
         y = lax.rem(yc + d, SIDE) if along_y else yc
         z = zc if along_y else lax.rem(zc + d, SIDE)
         if stage == 0:
-            ref = wcat.at[1, zc, half, :, block_cols]
+            ref = wcat.at[w, zc, half, :, block_cols]
         elif along_y:
-            ref = wcat.at[1, :, half, :, block_cols]
+            ref = wcat.at[w, :, half, :, block_cols]
         else:
-            ref = wcat.at[1, zc, half, :, side_cols(core)]
+            ref = wcat.at[w, zc, half, :, side_cols(core)]
         send, take = (s1_send, s1_recv) if stage == 0 else (s2_send, s2_recv)
         return pltpu.make_async_remote_copy(
             src_ref=ref,
             dst_ref=ref,
-            send_sem=send.at[half, d - 1],
-            recv_sem=take.at[half, d - 1],
+            send_sem=send.at[w - 1, half, d - 1],
+            recv_sem=take.at[w - 1, half, d - 1],
             device_id=(sec, row_at(z, y)),
             device_id_type=MESH,
         )
 
-    def join_copy(half, who):
-        ref = wcat.at[1, :, half, :, side_cols(who)]
+    def join_copy(w, half, who):
+        ref = wcat.at[w, :, half, :, side_cols(who)]
         return pltpu.make_async_remote_copy(
             src_ref=ref,
             dst_ref=ref,
-            send_sem=join_send.at[half],
-            recv_sem=join_recv.at[half],
+            send_sem=join_send.at[w - 1, half],
+            recv_sem=join_recv.at[w - 1, half],
             device_id=(sec, partner),
             device_id_type=MESH,
         )
 
-    def plane_one():
-        @pl.when(sec != 1)
-        def _():
-            deal_copy(0).wait_recv()
+    def plane_one(w):
+        @pl.when(sec != w)
+        def _():
+            deal_copy(w, 0).wait_recv()
             for half in range(2):
                 for d in range(1, SIDE):
-                    line_copy(0, half, d).start()
-
-    def plane_two():
-        @pl.when(sec != 1)
+                    line_copy(w, 0, half, d).start()
+
+    def plane_two(w, half):
+        @pl.when(sec != w)
+        def _():
+            for d in range(1, SIDE):
+                line_copy(w, 0, half, d).wait_recv()
+            for d in range(1, SIDE):
+                line_copy(w, 1, half, d).start()
+
+    def plane_three(w, half):
+        @pl.when(sec != w)
+        def _():
+            for d in range(1, SIDE):
+                line_copy(w, 1, half, d).wait_recv()
+            join_copy(w, half, core).start()
+
+    def plane_settle(w):
+        @pl.when(sec != w)
+        def _():
+            for half in range(2):
+                join_copy(w, half, 1 - core).wait_recv()
+
+    def plane_drain(w):
+        @pl.when(sec != w)
         def _():
             for half in range(2):
                 for d in range(1, SIDE):
-                    line_copy(0, half, d).wait_recv()
-                for d in range(1, SIDE):
-                    line_copy(1, half, d).start()
-
-    def plane_three():
-        @pl.when(sec != 1)
-        def _():
-            for half in range(2):
-                for d in range(1, SIDE):
-                    line_copy(1, half, d).wait_recv()
-                join_copy(half, core).start()
-
-    def plane_settle():
-        @pl.when(sec != 1)
-        def _():
-            for half in range(2):
-                join_copy(half, 1 - core).wait_recv()
-
-    def plane_drain():
-        @pl.when(sec != 1)
-        def _():
-            for half in range(2):
-                for d in range(1, SIDE):
-                    line_copy(0, half, d).wait_send()
-                    line_copy(1, half, d).wait_send()
-                join_copy(half, core).wait_send()
-
-        @pl.when(sec == 1)
+                    line_copy(w, 0, half, d).wait_send()
+                    line_copy(w, 1, half, d).wait_send()
+                join_copy(w, half, core).wait_send()
+
+        @pl.when(sec == w)
         def _():
             for d in range(1, LAYERS):
-                deal_copy(d).wait_send()
+                deal_copy(w, d).wait_send()
 
     def rows_of(k):
         return pl.ds(pl.multiple_of(k * piece, 16), piece)
+
+    def half_rows(who):
+        return pl.ds(pl.multiple_of(who * (n_chip * piece), 16), n_chip * piece)
+
+    own_block = rows_of(core * n_chip + chip)
 
     def split_block(a0, a1):
         top = jnp.concatenate([a0 * low, a1 * low], axis=1)
@@ -401,39 +428,65 @@
                 out = factor * out
             part[pl.ds(2 * SEQ * p, 2 * SEQ), :] = out.astype(BF)
 
+    def level_copy():
+        return pltpu.make_async_remote_copy(
+            src_ref=part.at[half_rows(1 - core)],
+            dst_ref=other,
+            send_sem=level_sem.at[0],
+            recv_sem=level_sem.at[1],
+            device_id=(sec, partner),
+            device_id_type=MESH,
+        )
+
     def rs_copy(d):
-        peer = lax.rem(me + d, n_row)
-        return pltpu.make_async_remote_copy(
-            src_ref=part.at[rows_of(peer)],
+        to = lax.rem(chip + d, n_chip)
+        return pltpu.make_async_remote_copy(
+            src_ref=both.at[rows_of(to)],
             dst_ref=recv.at[d],
             send_sem=rs_send.at[d],
             recv_sem=rs_recv.at[d],
-            device_id=(sec, peer),
+            device_id=(sec, 2 * to + core),
             device_id_type=MESH,
         )
 
     def start_reduce():
+        level_copy().start()
+        mine = part[half_rows(core), :].astype(F32)
+        level_copy().wait_recv()
+        both[...] = (mine + other[...].astype(F32)).astype(BF)
+
         def send(d, carry):
             rs_copy(d).start()
             return carry
 
-        lax.fori_loop(1, n_row, send, 0)
+        lax.fori_loop(1, n_chip, send, 0)
 
     def finish_reduce():
         def take(d, total):
             rs_copy(d).wait_recv()
             return total + recv[d].astype(F32)
 
-        return lax.fori_loop(1, n_row, take, part[rows_of(me), :].astype(F32))
+        return lax.fori_loop(1, n_chip, take, both[rows_of(chip), :].astype(F32))
 
     def ag_copy(buf, d):
-        peer = lax.rem(me + d, n_row)
-        return pltpu.make_async_remote_copy(
-            src_ref=buf.at[rows_of(me)],
-            dst_ref=buf.at[rows_of(me)],
+        to = lax.rem(chip + d, n_chip)
+        return pltpu.make_async_remote_copy(
+            src_ref=buf.at[own_block],
+            dst_ref=buf.at[own_block],
             send_sem=ag_send.at[d],
             recv_sem=ag_recv.at[d],
-            device_id=(sec, peer),
+            device_id=(sec, 2 * to + core),
+            device_id_type=MESH,
+        )
+
+    def hand_copy(buf, d):
+        block = rows_of(core * n_chip + lax.rem(chip + n_chip - d, n_chip))
+        return pltpu.make_async_remote_copy(
+            src_ref=buf.at[block],
+            dst_ref=buf.at[block],
+            send_sem=hand_send.at[d],
+            recv_sem=hand_recv.at[d],
+            device_id=(sec, partner),
             device_id_type=MESH,
         )
 
@@ -442,16 +495,31 @@
             ag_copy(buf, d).start()
             return carry
 
-        lax.fori_loop(1, n_row, send, 0)
+        lax.fori_loop(1, n_chip, send, 0)
+        hand_copy(buf, 0).start()
 
     def finish_gather(buf):
         def take(d, carry):
             ag_copy(buf, d).wait_recv()
+            hand_copy(buf, d).start()
+            return carry
+
+        lax.fori_loop(1, n_chip, take, 0)
+
+        def settle_one(d, carry):
+            hand_copy(buf, d).wait_recv()
+            hand_copy(buf, d).wait_send()
+            return carry
+
+        lax.fori_loop(0, n_chip, settle_one, 0)
+
+        def sent(d, carry):
             rs_copy(d).wait_send()
             ag_copy(buf, d).wait_send()
             return carry
 
-        lax.fori_loop(1, n_row, take, 0)
+        lax.fori_loop(1, n_chip, sent, 0)
+        level_copy().wait_send()
 
     def halves(ref, base, p):
         cols = pl.ds(base + SEQ * p, SEQ)
@@ -538,8 +606,8 @@
         pair_copy(u, par).wait_recv()
         pair_copy(u, par).wait_send()
         for z in range(SIDE):
-            both = grad[u, core, z].astype(F32) + pairbuf[par, u, z].astype(F32)
-            grad[u, core, z] = both.astype(BF)
+            total = grad[u, core, z].astype(F32) + pairbuf[par, u, z].astype(F32)
+            grad[u, core, z] = total.astype(BF)
         for d in range(1, SIDE):
             c1_copy(u, par, d).start()
 
@@ -580,13 +648,19 @@
             xout[u] = total.astype(BF)
             x_copy(u, t).start()
 
-    @pl.when(sec == 1)
+    for w in (1, 2):
+
+        @pl.when(sec == w)
+        def _():
+            for d in range(1, LAYERS):
+                deal_copy(w, d).start()
+
+    @pl.when(sec == 0)
     def _():
-        for d in range(1, LAYERS):
-            deal_copy(d).start()
-
-    launch_flow(0, True)
-    launch_flow(2)
+        for t in (1, 3, 2):
+            first_copy(t).start()
+
+    launch_flow()
 
     def forward(l, carry):
         here = qkv.at[l]
@@ -608,8 +682,9 @@
 
         @pl.when(l > 0)
         def _():
-            pl.when(l == 1)(plane_settle)
-            pl.when(l > 1)(lambda: settle(l))
+            for w in (1, 2):
+                pl.when(l == w)(functools.partial(plane_settle, w))
+            pl.when(l == RING)(settle)
             normal, _ = norm_parts(xs[l])
             h = (normal * gains[l]).astype(BF)
             for n in range(3):
@@ -621,45 +696,33 @@
 
         @pl.when(l == 0)
         def _():
-            plane_one()
-            for slot in range(1, CHUNKS_FIRST + 3):
-                pump(0, slot, True)
-            for slot in range(1, 4):
-                pump(2, slot)
+            plane_one(1)
+            plane_two(1, 0)
 
         @pl.when(l == 1)
         def _():
-            for slot in range(7, CHUNKS + 3):
-                pump(2, slot)
-
-        @pl.when(l == 2)
-        def _():
-            for slot in range(4, 7):
-                pump(3, slot)
+            plane_two(2, 0)
+
+        for turn in range(3):
+            pl.when(l == turn)(functools.partial(pump, 2 * turn + 1))
 
         logits = finish_reduce()
         shifted = jnp.exp(logits - jnp.max(logits, axis=-1, keepdims=True))
         own = shifted / jnp.sum(shifted, axis=-1, keepdims=True)
         probs_l = probs.at[l]
-        probs_l[rows_of(me), :] = own.astype(BF)
+        probs_l[own_block, :] = own.astype(BF)
         start_gather(probs_l)
 
         @pl.when(l == 0)
         def _():
-            plane_two()
-            for slot in range(4, 7):
-                pump(2, slot)
-            launch_flow(3)
+            plane_two(1, 1)
 
         @pl.when(l == 1)
         def _():
-            for slot in range(1, 4):
-                pump(3, slot)
-
-        @pl.when(l == 2)
-        def _():
-            for slot in range(7, CHUNKS + 3):
-                pump(3, slot)
+            plane_two(2, 1)
+
+        for turn in range(2):
+            pl.when(l == turn)(functools.partial(pump, 2 * turn + 2))
 
         finish_gather(probs_l)
         mixed_l = mixed.at[l]
@@ -669,12 +732,33 @@
 
         @pl.when(l == 0)
         def _():
-            plane_three()
-            settle(0, True)
+            @pl.when(sec > 0)
+            def _():
+                first_copy(0).wait_recv()
+                first_twin(core).start()
+
+            plane_three(1, 0)
+
+            @pl.when(sec > 0)
+            def _():
+                first_twin(1 - core).wait_recv()
+
+        @pl.when(l == 1)
+        def _():
+            plane_three(2, 0)
 
         @pl.when(l < LAYERS - 1)
         def _():
             xs[l + 1] = xs[l] + dot(mixed_l[...], weight(l, 3 * WIDTH, WIDTH), 1, 0)
+
+        @pl.when(l == 0)
+        def _():
+            plane_three(1, 1)
+            plane_one(2)
+
+        @pl.when(l == 1)
+        def _():
+            plane_three(2, 1)
 
         return carry
 
@@ -733,9 +817,9 @@
             out = dot(probs_l[rows, :], split_block(*halves(dmix, 0, p)), 0, 0)
             put_halves(dqkv, 2 * WIDTH, p, out.astype(BF))
         dprobs = finish_reduce()
-        own = probs_l[rows_of(me), :].astype(F32)
+        own = probs_l[own_block, :].astype(F32)
         inner = jnp.sum(dprobs * own, axis=-1, keepdims=True)
-        dlog[rows_of(me), :] = (own * (dprobs - inner)).astype(BF)
+        dlog[own_block, :] = (own * (dprobs - inner)).astype(BF)
         start_gather(dlog)
 
         normal, rstd = norm_parts(xs[l])
@@ -802,19 +886,20 @@
         else:
             gq_ref[0, :, pl.ds(WIDTH * {VAL: 2, QRY: 0, KEY: 1}[u], WIDTH)] = total
 
-    drain(0, True)
-    for l in range(2, LAYERS):
-        drain(l)
-    plane_drain()
+    drain()
+    for w in (1, 2):
+        plane_drain(w)
 
     @pl.when(sec == 0)
     def _():
         for t in range(1, LAYERS):
             tab_copy(t).wait_send()
+            first_copy(t).wait_send()
 
     @pl.when(sec > 0)
     def _():
         tab_twin(core).wait_send()
+        first_twin(core).wait_send()
 
     for d in range(1, LAYERS):
         gain_copy(d).wait_send()
@@ -850,7 +935,9 @@
             pltpu.VMEM((LAYERS, flat, seq), BF),
             pltpu.VMEM((LAYERS, npos, width), BF),
             pltpu.VMEM((flat, seq), BF),
-            pltpu.VMEM((n_row, flat // n_row, seq), BF),
+            pltpu.VMEM((flat // 2, seq), BF),
+            pltpu.VMEM((flat // 2, seq), BF),
+            pltpu.VMEM((n_row // 2, flat // n_row, seq), BF),
             pltpu.VMEM((flat, seq), BF),
             pltpu.VMEM((npos, width), F32),
             pltpu.VMEM((npos, width), BF),
@@ -866,28 +953,33 @@
             pltpu.VMEM((4, own_rows, width), BF),
             pltpu.VMEM((4, LAYERS - 1, own_rows, width), BF),
             pltpu.VMEM((4, own_rows, width), F32),
-            dma((n_row,)),
-            dma((n_row,)),
-            dma((n_row,)),
-            dma((n_row,)),
+            dma((2,)),
+            dma((n_row // 2,)),
+            dma((n_row // 2,)),
+            dma((n_row // 2,)),
+            dma((n_row // 2,)),
+            dma((n_row // 2,)),
+            dma((n_row // 2,)),
             dma((2,)),
             dma,
             dma((LAYERS,)),
             dma((2,)),
             dma((LAYERS,)),
             dma((LAYERS,)),
+            dma((2, LAYERS)),
+            dma((2,)),
+            dma((2, 2, SIDE - 1)),
+            dma((2, 2, SIDE - 1)),
+            dma((2, 2, SIDE - 1)),
+            dma((2, 2, SIDE - 1)),
+            dma((2, 2)),
+            dma((2, 2)),
+            dma((2, CHUNKS)),
+            dma((2, CHUNKS)),
+            dma((2, CHUNKS)),
+            dma((2, CHUNKS)),
             dma((LAYERS,)),
-            dma,
-            dma((2, SIDE - 1)),
-            dma((2, SIDE - 1)),
-            dma((2, SIDE - 1)),
-            dma((2, SIDE - 1)),
             dma((2,)),
-            dma((2,)),
-            dma((LAYERS, 2, CHUNKS)),
-            dma((LAYERS, 2, CHUNKS)),
-            dma((LAYERS, 2, CHUNKS)),
-            dma((LAYERS, 2, CHUNKS)),
             dma((4,)),
             dma((2, 4)),
             dma((4, SIDE - 1)),

time: 272 us -> 236 us (0.87)
  Pallas kernels: 266 us -> 229 us
    pallas_call x1, Pallas kernels: 266 us -> 229 us  [local(): pl.pallas_call(functools.partial(kernel, n_row, scale), out_shape=(jax.Sh...]
where the time goes in v4:
time: 236 us; the launch traced here: 235 us
  Pallas kernels  229 us (97%)
  local copies, waits for them, and re-layouts  3.15 us (1%)
  other arithmetic  2.42 us (1%)
    pallas_call x1, Pallas kernels, local(): pl.pallas_call(functools.partial(kernel, n_row, scale), out_shape=(jax.Sh...  229 us

profile of v4, /device:TPU:0, one launch (start us, length us, event | category | flops | bytes accessed | tf_op | source)
XLA Modules:
  0.0 235.4 jit_solution(16602454016451066840)
XLA Ops:
  0.6 229.2 %shard_map.85 = (f32[1,24,2304]{2,1,0:T(8,128)}, f32[1,24,768]{2,1,0:T(8,128)}) custom-call(s32[4,2,128]{2,1,0:T(2,128)} %tok_ref.1, bf16[33,768]{1,0:T(8,128)(2,1)} %emb_ref.1, f32[1,768]{1,0:T(1,128)} %gain_ref.1, bf16[4,2,96,2304]{3,2,1,0:T(8,128)(2,1)} %bitcast.5, bf16[4,2,96,768]{3,2,1,0:T(8,128)(2,1)} %bitcast.7, bf16[4,256,768]{2,1,0:T(8,128)(2,1)} %bitcast.6), custom_call_target="tpu_custom_call" | custom-call | tf_op jit(solution)/shard_map/pallas_call | solution.py:920
  229.9 1.1 multiply_reduce_fusion
  231.0 1.3 bitcast_divide_fusion
  232.3 1.6 copy.11
  233.9 1.5 copy.12

commit v5 on v4

--- a/solution.py
+++ b/solution.py
@@ -45,6 +45,7 @@
     og_hbm,
     gq_ref,
     go_ref,
+    gg_ref,
     wcat,
     gains,
     embp,
@@ -87,6 +88,8 @@
     gain_recv,
     deal_send,
     deal_recv,
+    bulk_send,
+    bulk_recv,
     s1_send,
     s1_recv,
     s2_send,
@@ -323,13 +326,25 @@
         return pl.ds(pl.multiple_of(who * (2 * WIDTH), 128), 2 * WIDTH)
 
     def deal_copy(w, d):
-        ref = wcat.at[w, zc, :, :, block_cols]
+        halves_sent = 2 if w == 1 else 1
+        ref = wcat.at[w, zc, pl.ds(0, halves_sent), :, block_cols]
         return pltpu.make_async_remote_copy(
             src_ref=ref,
             dst_ref=ref,
             send_sem=deal_send.at[w - 1, d],
             recv_sem=deal_recv.at[w - 1],
             device_id=((w + d) % LAYERS, me),
+            device_id_type=MESH,
+        )
+
+    def bulk_copy(d):
+        ref = wcat.at[2, :, 1, :, side_cols(core)]
+        return pltpu.make_async_remote_copy(
+            src_ref=ref,
+            dst_ref=ref,
+            send_sem=bulk_send.at[d],
+            recv_sem=bulk_recv,
+            device_id=((2 + d) % LAYERS, me),
             device_id_type=MESH,
         )
 
@@ -368,7 +383,7 @@
         @pl.when(sec != w)
         def _():
             deal_copy(w, 0).wait_recv()
-            for half in range(2):
+            for half in range(2 if w == 1 else 1):
                 for d in range(1, SIDE):
                     line_copy(w, 0, half, d).start()
 
@@ -383,8 +398,11 @@
     def plane_three(w, half):
         @pl.when(sec != w)
         def _():
-            for d in range(1, SIDE):
-                line_copy(w, 1, half, d).wait_recv()
+            if w == 2 and half == 1:
+                bulk_copy(0).wait_recv()
+            else:
+                for d in range(1, SIDE):
+                    line_copy(w, 1, half, d).wait_recv()
             join_copy(w, half, core).start()
 
     def plane_settle(w):
@@ -398,14 +416,17 @@
         def _():
             for half in range(2):
                 for d in range(1, SIDE):
-                    line_copy(w, 0, half, d).wait_send()
-                    line_copy(w, 1, half, d).wait_send()
+                    if w == 1 or half == 0:
+                        line_copy(w, 0, half, d).wait_send()
+                        line_copy(w, 1, half, d).wait_send()
                 join_copy(w, half, core).wait_send()
 
         @pl.when(sec == w)
         def _():
             for d in range(1, LAYERS):
                 deal_copy(w, d).wait_send()
+                if w == 2:
+                    bulk_copy(d).wait_send()
 
     def rows_of(k):
         return pl.ds(pl.multiple_of(k * piece, 16), piece)
@@ -654,6 +675,9 @@
         def _():
             for d in range(1, LAYERS):
                 deal_copy(w, d).start()
+            if w == 2:
+                for d in (1, 3, 2):
+                    bulk_copy(d).start()
 
     @pl.when(sec == 0)
     def _():
@@ -716,10 +740,7 @@
         @pl.when(l == 0)
         def _():
             plane_two(1, 1)
-
-        @pl.when(l == 1)
-        def _():
-            plane_two(2, 1)
+            plane_one(2)
 
         for turn in range(2):
             pl.when(l == turn)(functools.partial(pump, 2 * turn + 2))
@@ -754,7 +775,6 @@
         @pl.when(l == 0)
         def _():
             plane_three(1, 1)
-            plane_one(2)
 
         @pl.when(l == 1)
         def _():
@@ -886,6 +906,18 @@
         else:
             gq_ref[0, :, pl.ds(WIDTH * {VAL: 2, QRY: 0, KEY: 1}[u], WIDTH)] = total
 
+    tall = wcat[sec, zc, yc // 2, pl.ds(pl.multiple_of(2 * own_rows * lax.rem(yc, 2), 16), 2 * own_rows), :]
+    tall = tall[:, : 3 * WIDTH].astype(F32)
+    w_own = jnp.where(core == 0, tall[:own_rows], tall[own_rows:])
+    dotted = jnp.sum(w_own * gq_ref[0], axis=-1, keepdims=True)
+    lanes = lax.broadcasted_iota(jnp.int32, (own_rows, WIDTH), 1)
+    subs = lax.broadcasted_iota(jnp.int32, (own_rows, WIDTH), 0)
+    gain_own = jnp.sum(
+        jnp.where(lanes == subs + own_rows * me, gain_ref[...], 0.0), axis=-1, keepdims=True
+    )
+    spread = jnp.where(lanes == subs, dotted / gain_own, 0.0)
+    gg_ref[...] = jnp.sum(spread, axis=0, keepdims=True)[:, :own_rows]
+
     drain()
     for w in (1, 2):
         plane_drain(w)
@@ -905,9 +937,14 @@
         gain_copy(d).wait_send()
 
 
+def hand_over(qkv_in, out_in, gain_in, qkv_out, out_out, gain_out):
+    qkv_out[...] = qkv_in[...]
+    out_out[...] = out_in[...]
+    gain_out[...] = gain_in[...]
+
+
 def local(tokens, embed, ln_gain, w_qkv, w_out, out_grad):
     n_row = lax.axis_size("row")
-    row = lax.axis_index("row")
     micro, rows_here, seq = tokens.shape
     vocab, width = embed.shape
     npos = rows_here * seq
@@ -917,14 +954,15 @@
     own_rows = width // n_row
     vm, anyspace = pl.BlockSpec(memory_space=pltpu.VMEM), pl.BlockSpec(memory_space=pl.ANY)
     dma = pltpu.SemaphoreType.DMA
-    grad_qkv, grad_out = pl.pallas_call(
+    sums = pl.pallas_call(
         functools.partial(kernel, n_row, scale),
         out_shape=(
             jax.ShapeDtypeStruct((1, own_rows, 3 * width), F32),
             jax.ShapeDtypeStruct((1, own_rows, width), F32),
+            jax.ShapeDtypeStruct((1, own_rows), F32),
         ),
         in_specs=[vm, vm, vm, anyspace, anyspace, anyspace],
-        out_specs=(vm, vm),
+        out_specs=(vm, vm, vm),
         scratch_shapes=[
             pltpu.VMEM((LAYERS, SIDE, 2, width // 8, 4 * width), BF),
             pltpu.VMEM((LAYERS, 1, width), F32),
@@ -968,6 +1006,8 @@
             dma((LAYERS,)),
             dma((2, LAYERS)),
             dma((2,)),
+            dma((LAYERS,)),
+            dma,
             dma((2, 2, SIDE - 1)),
             dma((2, 2, SIDE - 1)),
             dma((2, 2, SIDE - 1)),
@@ -1000,9 +1040,12 @@
         w_out.reshape(SIDE, 2, width // 8, width),
         out_grad.reshape(micro, npos, width),
     )
-    w_own = lax.dynamic_slice_in_dim(w_qkv[0], row * own_rows, own_rows, 0).astype(F32)
-    gain_own = lax.dynamic_slice_in_dim(ln_gain[0], row * own_rows, own_rows, 0)
-    grad_gain = (jnp.sum(w_own * grad_qkv[0], axis=-1) / gain_own)[None]
+    grad_qkv, grad_out, grad_gain = pl.pallas_call(
+        hand_over,
+        out_shape=tuple(jax.ShapeDtypeStruct(g.shape, F32) for g in sums),
+        in_specs=[vm, vm, vm],
+        out_specs=(vm, vm, vm),
+    )(*sums)
     return (grad_qkv, grad_out, grad_gain)
 
 

time: 236 us -> 231 us (0.979)
  local copies, waits for them, and re-layouts: 3.15 us -> 0 us
  other arithmetic: 2.42 us -> 0 us
    unnamed x2 -> x0, local copies, waits for them, and re-layouts: 3.15 us -> none
where the time goes in v5:
time: 231 us
  Pallas kernels  230 us (100%)
    pallas_call x1, Pallas kernels, local(): pl.pallas_call(functools.partial(kernel, n_row, scale), out_shape=(jax.Sh...  229 us

profile of v5, /device:TPU:0, one launch (start us, length us, event | category | flops | bytes accessed | tf_op | source)
XLA Modules:
  0.0 231.0 jit_solution(6918124458979668424)
XLA Ops:
  0.6 228.7 %shard_map.85 = (f32[1,24,2304]{2,1,0:T(8,128)}, f32[1,24,768]{2,1,0:T(8,128)}, f32[1,24]{1,0:T(1,128)}) custom-call(s32[4,2,128]{2,1,0:T(2,128)} %tok_ref.1, bf16[33,768]{1,0:T(8,128)(2,1)} %emb_ref.1, f32[1,768]{1,0:T(1,128)} %gain_ref.1, bf16[4,2,96,2304]{3,2,1,0:T(8,128)(2,1)} %bitcast.3, bf16[4,2,96,768]{3,2,1,0:T(8,128)(2,1)} %bitcast.5, ...), custom_call_target="tpu_custom_call" | custom-call | tf_op jit(solution)/shard_map/pallas_call | solution.py:957
  229.4 1.7 shard_map.86

commit v6 on v5

--- a/solution.py
+++ b/solution.py
@@ -16,6 +16,10 @@
 SIDE = 4
 OUT, VAL, QRY, KEY = 0, 1, 2, 3
 CHUNKS = 3
+NEAR = sorted(
+    ((z, y) for z in range(SIDE) for y in range(SIDE) if z or y),
+    key=lambda step: sum(min(n, SIDE - n) for n in step),
+)
 CHUNK = 4 * WIDTH // CHUNKS
 HALF = WIDTH // 2
 MESH = pl.DeviceIdType.MESH
@@ -459,8 +463,12 @@
             device_id_type=MESH,
         )
 
+    def chip_at(step, sign):
+        z, y = ((sign * n) % SIDE for n in step)
+        return lax.rem(zc + z, SIDE) * SIDE + lax.rem(yc + y, SIDE)
+
     def rs_copy(d):
-        to = lax.rem(chip + d, n_chip)
+        to = chip_at(NEAR[d - 1], 1)
         return pltpu.make_async_remote_copy(
             src_ref=both.at[rows_of(to)],
             dst_ref=recv.at[d],
@@ -475,22 +483,18 @@
         mine = part[half_rows(core), :].astype(F32)
         level_copy().wait_recv()
         both[...] = (mine + other[...].astype(F32)).astype(BF)
-
-        def send(d, carry):
+        for d in reversed(range(1, n_chip)):
             rs_copy(d).start()
-            return carry
-
-        lax.fori_loop(1, n_chip, send, 0)
 
     def finish_reduce():
-        def take(d, total):
+        total = both[rows_of(chip), :].astype(F32)
+        for d in range(1, n_chip):
             rs_copy(d).wait_recv()
-            return total + recv[d].astype(F32)
-
-        return lax.fori_loop(1, n_chip, take, both[rows_of(chip), :].astype(F32))
+            total = total + recv[d].astype(F32)
+        return total
 
     def ag_copy(buf, d):
-        to = lax.rem(chip + d, n_chip)
+        to = chip_at(NEAR[d - 1], 1)
         return pltpu.make_async_remote_copy(
             src_ref=buf.at[own_block],
             dst_ref=buf.at[own_block],
@@ -501,7 +505,8 @@
         )
 
     def hand_copy(buf, d):
-        block = rows_of(core * n_chip + lax.rem(chip + n_chip - d, n_chip))
+        source = chip_at(NEAR[d - 1], -1) if d else chip
+        block = rows_of(core * n_chip + source)
         return pltpu.make_async_remote_copy(
             src_ref=buf.at[block],
             dst_ref=buf.at[block],
@@ -512,34 +517,23 @@
         )
 
     def start_gather(buf):
-        def send(d, carry):
+        for d in reversed(range(1, n_chip)):
             ag_copy(buf, d).start()
-            return carry
-
-        lax.fori_loop(1, n_chip, send, 0)
         hand_copy(buf, 0).start()
 
     def finish_gather(buf):
-        def take(d, carry):
+        for d in range(1, n_chip):
             ag_copy(buf, d).wait_recv()
             hand_copy(buf, d).start()
-            return carry
-
-        lax.fori_loop(1, n_chip, take, 0)
-
-        def settle_one(d, carry):
+        for d in range(n_chip):
             hand_copy(buf, d).wait_recv()
+
+    def clear_exchange(buf):
+        for d in range(n_chip):
             hand_copy(buf, d).wait_send()
-            return carry
-
-        lax.fori_loop(0, n_chip, settle_one, 0)
-
-        def sent(d, carry):
+        for d in range(1, n_chip):
             rs_copy(d).wait_send()
             ag_copy(buf, d).wait_send()
-            return carry
-
-        lax.fori_loop(1, n_chip, sent, 0)
         level_copy().wait_send()
 
     def halves(ref, base, p):
@@ -684,8 +678,6 @@
         for t in (1, 3, 2):
             first_copy(t).start()
 
-    launch_flow()
-
     def forward(l, carry):
         here = qkv.at[l]
 
@@ -708,7 +700,12 @@
         def _():
             for w in (1, 2):
                 pl.when(l == w)(functools.partial(plane_settle, w))
-            pl.when(l == RING)(settle)
+
+            @pl.when(l == RING)
+            def _():
+                pump(5)
+                settle()
+
             normal, _ = norm_parts(xs[l])
             h = (normal * gains[l]).astype(BF)
             for n in range(3):
@@ -727,8 +724,8 @@
         def _():
             plane_two(2, 0)
 
-        for turn in range(3):
-            pl.when(l == turn)(functools.partial(pump, 2 * turn + 1))
+        for turn in (1, 2):
+            pl.when(l == turn)(functools.partial(pump, 2 * turn - 1))
 
         logits = finish_reduce()
         shifted = jnp.exp(logits - jnp.max(logits, axis=-1, keepdims=True))
@@ -741,11 +738,13 @@
         def _():
             plane_two(1, 1)
             plane_one(2)
-
-        for turn in range(2):
-            pl.when(l == turn)(functools.partial(pump, 2 * turn + 2))
+            launch_flow()
+
+        for turn in (1, 2):
+            pl.when(l == turn)(functools.partial(pump, 2 * turn))
 
         finish_gather(probs_l)
+        clear_exchange(probs_l)
         mixed_l = mixed.at[l]
         for p in range(PAIRS):
             out = dot(beside(probs_l, p), split_block(*halves(here, 2 * WIDTH, p)), 1, 0)
@@ -858,6 +857,7 @@
 
         pl.when(step >= 2)(older)
         finish_gather(dlog)
+        clear_exchange(dlog)
 
         for p in range(PAIRS):
             out = dot(beside(dlog, p), split_block(*halves(here, WIDTH, p)), 1, 0)

time: 231 us -> 239 us (1.035)
  Pallas kernels: 230 us -> 238 us
    pallas_call x1, Pallas kernels: 229 us -> 237 us  [local(): pl.pallas_call(functools.partial(kernel, n_row, scale), out_shape=(jax.Sh...]
where the time goes in v6:
time: 239 us
  Pallas kernels  238 us (100%)
    pallas_call x1, Pallas kernels, local(): pl.pallas_call(functools.partial(kernel, n_row, scale), out_shape=(jax.Sh...  237 us

profile of v6, /device:TPU:0, one launch (start us, length us, event | category | flops | bytes accessed | tf_op | source)
XLA Modules:
  0.0 239.1 jit_solution(4315282836557062578)
XLA Ops:
  0.6 236.8 %shard_map.85 = (f32[1,24,2304]{2,1,0:T(8,128)}, f32[1,24,768]{2,1,0:T(8,128)}, f32[1,24]{1,0:T(1,128)}) custom-call(s32[4,2,128]{2,1,0:T(2,128)} %tok_ref.1, bf16[33,768]{1,0:T(8,128)(2,1)} %emb_ref.1, f32[1,768]{1,0:T(1,128)} %gain_ref.1, bf16[4,2,96,2304]{3,2,1,0:T(8,128)(2,1)} %bitcast.3, bf16[4,2,96,768]{3,2,1,0:T(8,128)(2,1)} %bitcast.5, ...), custom_call_target="tpu_custom_call" | custom-call | tf_op jit(solution)/shard_map/pallas_call | solution.py:957
  237.4 1.7 shard_map.86

commit v7 on v6

--- a/solution.py
+++ b/solution.py
@@ -92,8 +92,6 @@
     gain_recv,
     deal_send,
     deal_recv,
-    bulk_send,
-    bulk_recv,
     s1_send,
     s1_recv,
     s2_send,
@@ -227,7 +225,7 @@
 
     def flow(d, k, who):
         cols = pl.ds(pl.multiple_of(k * CHUNK, 128), CHUNK)
-        return wcat.at[RING, who * 2 + d, :, :, cols]
+        return wcat.at[RING, who * 2 + d, 1, :, cols]
 
     def place(d):
         return lax.rem(sec - RING + LAYERS, LAYERS) if d == 0 else lax.rem(RING - sec, LAYERS)
@@ -329,26 +327,17 @@
     def side_cols(who):
         return pl.ds(pl.multiple_of(who * (2 * WIDTH), 128), 2 * WIDTH)
 
+    def parts_of(w):
+        return 1 if w == RING else 2
+
     def deal_copy(w, d):
-        halves_sent = 2 if w == 1 else 1
-        ref = wcat.at[w, zc, pl.ds(0, halves_sent), :, block_cols]
+        ref = wcat.at[w, zc, pl.ds(0, parts_of(w)), :, block_cols]
         return pltpu.make_async_remote_copy(
             src_ref=ref,
             dst_ref=ref,
             send_sem=deal_send.at[w - 1, d],
             recv_sem=deal_recv.at[w - 1],
             device_id=((w + d) % LAYERS, me),
-            device_id_type=MESH,
-        )
-
-    def bulk_copy(d):
-        ref = wcat.at[2, :, 1, :, side_cols(core)]
-        return pltpu.make_async_remote_copy(
-            src_ref=ref,
-            dst_ref=ref,
-            send_sem=bulk_send.at[d],
-            recv_sem=bulk_recv,
-            device_id=((2 + d) % LAYERS, me),
             device_id_type=MESH,
         )
 
@@ -387,7 +376,7 @@
         @pl.when(sec != w)
         def _():
             deal_copy(w, 0).wait_recv()
-            for half in range(2 if w == 1 else 1):
+            for half in range(parts_of(w)):
                 for d in range(1, SIDE):
                     line_copy(w, 0, half, d).start()
 
@@ -402,35 +391,29 @@
     def plane_three(w, half):
         @pl.when(sec != w)
         def _():
-            if w == 2 and half == 1:
-                bulk_copy(0).wait_recv()
-            else:
-                for d in range(1, SIDE):
-                    line_copy(w, 1, half, d).wait_recv()
+            for d in range(1, SIDE):
+                line_copy(w, 1, half, d).wait_recv()
             join_copy(w, half, core).start()
 
     def plane_settle(w):
         @pl.when(sec != w)
         def _():
-            for half in range(2):
+            for half in range(parts_of(w)):
                 join_copy(w, half, 1 - core).wait_recv()
 
     def plane_drain(w):
         @pl.when(sec != w)
         def _():
-            for half in range(2):
+            for half in range(parts_of(w)):
                 for d in range(1, SIDE):
-                    if w == 1 or half == 0:
-                        line_copy(w, 0, half, d).wait_send()
-                        line_copy(w, 1, half, d).wait_send()
+                    line_copy(w, 0, half, d).wait_send()
+                    line_copy(w, 1, half, d).wait_send()
                 join_copy(w, half, core).wait_send()
 
         @pl.when(sec == w)
         def _():
             for d in range(1, LAYERS):
                 deal_copy(w, d).wait_send()
-                if w == 2:
-                    bulk_copy(d).wait_send()
 
     def rows_of(k):
         return pl.ds(pl.multiple_of(k * piece, 16), piece)
@@ -663,20 +646,19 @@
             xout[u] = total.astype(BF)
             x_copy(u, t).start()
 
-    for w in (1, 2):
+    for w in (1, 2, 3):
 
         @pl.when(sec == w)
         def _():
             for d in range(1, LAYERS):
                 deal_copy(w, d).start()
-            if w == 2:
-                for d in (1, 3, 2):
-                    bulk_copy(d).start()
 
     @pl.when(sec == 0)
     def _():
         for t in (1, 3, 2):
             first_copy(t).start()
+
+    launch_flow()
 
     def forward(l, carry):
         here = qkv.at[l]
@@ -698,12 +680,11 @@
 
         @pl.when(l > 0)
         def _():
-            for w in (1, 2):
+            for w in (1, 2, 3):
                 pl.when(l == w)(functools.partial(plane_settle, w))
 
             @pl.when(l == RING)
             def _():
-                pump(5)
                 settle()
 
             normal, _ = norm_parts(xs[l])
@@ -724,8 +705,12 @@
         def _():
             plane_two(2, 0)
 
-        for turn in (1, 2):
-            pl.when(l == turn)(functools.partial(pump, 2 * turn - 1))
+        @pl.when(l == 2)
+        def _():
+            plane_two(3, 0)
+
+        for turn in range(3):
+            pl.when(l == turn)(functools.partial(pump, 2 * turn + 1))
 
         logits = finish_reduce()
         shifted = jnp.exp(logits - jnp.max(logits, axis=-1, keepdims=True))
@@ -738,10 +723,14 @@
         def _():
             plane_two(1, 1)
             plane_one(2)
-            launch_flow()
-
-        for turn in (1, 2):
-            pl.when(l == turn)(functools.partial(pump, 2 * turn))
+
+        @pl.when(l == 1)
+        def _():
+            plane_two(2, 1)
+            plane_one(3)
+
+        for turn in range(2):
+            pl.when(l == turn)(functools.partial(pump, 2 * turn + 2))
 
         finish_gather(probs_l)
         clear_exchange(probs_l)
@@ -778,6 +767,10 @@
         @pl.when(l == 1)
         def _():
             plane_three(2, 1)
+
+        @pl.when(l == 2)
+        def _():
+            plane_three(3, 0)
 
         return carry
 
@@ -919,7 +912,7 @@
     gg_ref[...] = jnp.sum(spread, axis=0, keepdims=True)[:, :own_rows]
 
     drain()
-    for w in (1, 2):
+    for w in (1, 2, 3):
         plane_drain(w)
 
     @pl.when(sec == 0)
@@ -1004,16 +997,14 @@
             dma((2,)),
             dma((LAYERS,)),
             dma((LAYERS,)),
-            dma((2, LAYERS)),
-            dma((2,)),
-            dma((LAYERS,)),
-            dma,
-            dma((2, 2, SIDE - 1)),
-            dma((2, 2, SIDE - 1)),
-            dma((2, 2, SIDE - 1)),
-            dma((2, 2, SIDE - 1)),
-            dma((2, 2)),
-            dma((2, 2)),
+            dma((3, LAYERS)),
+            dma((3,)),
+            dma((3, 2, SIDE - 1)),
+            dma((3, 2, SIDE - 1)),
+            dma((3, 2, SIDE - 1)),
+            dma((3, 2, SIDE - 1)),
+            dma((3, 2)),
+            dma((3, 2)),
             dma((2, CHUNKS)),
             dma((2, CHUNKS)),
             dma((2, CHUNKS)),

time: 239 us -> 237 us (level)
    pallas_call x1, Pallas kernels: 237 us -> 234 us  [local(): pl.pallas_call(functools.partial(kernel, n_row, scale), out_shape=(jax.Sh...]
where the time goes in v7:
time: 237 us; the launch traced here: 236 us
  Pallas kernels  236 us (100%)
    pallas_call x1, Pallas kernels, local(): pl.pallas_call(functools.partial(kernel, n_row, scale), out_shape=(jax.Sh...  234 us

profile of v7, /device:TPU:0, one launch (start us, length us, event | category | flops | bytes accessed | tf_op | source)
XLA Modules:
  0.0 236.4 jit_solution(15765039575809039791)
XLA Ops:
  0.6 234.1 %shard_map.85 = (f32[1,24,2304]{2,1,0:T(8,128)}, f32[1,24,768]{2,1,0:T(8,128)}, f32[1,24]{1,0:T(1,128)}) custom-call(s32[4,2,128]{2,1,0:T(2,128)} %tok_ref.1, bf16[33,768]{1,0:T(8,128)(2,1)} %emb_ref.1, f32[1,768]{1,0:T(1,128)} %gain_ref.1, bf16[4,2,96,2304]{3,2,1,0:T(8,128)(2,1)} %bitcast.3, bf16[4,2,96,768]{3,2,1,0:T(8,128)(2,1)} %bitcast.5, ...), custom_call_target="tpu_custom_call" | custom-call | tf_op jit(solution)/shard_map/pallas_call | solution.py:950
  234.7 1.7 shard_map.86

commit v8 on v6

--- a/solution.py
+++ b/solution.py
@@ -185,30 +185,46 @@
     local_out.wait()
     pl.semaphore_wait(barrier, n_chip + LAYERS - 1)
 
-    def tab_copy(t):
-        return pltpu.make_async_remote_copy(
-            src_ref=tab.at[core],
-            dst_ref=tab.at[core],
-            send_sem=tab_send.at[t],
-            recv_sem=tab_recv.at[0],
+    def tab_part(who, late):
+        return tab.at[who, :, pl.ds(2 * HALF, HALF) if late else pl.ds(0, 2 * HALF)]
+
+    def tab_copy(t, late):
+        return pltpu.make_async_remote_copy(
+            src_ref=tab_part(core, late),
+            dst_ref=tab_part(core, late),
+            send_sem=tab_send.at[late, t],
+            recv_sem=tab_recv.at[late, 0],
             device_id=(t, me),
             device_id_type=MESH,
         )
 
-    def tab_twin(who):
-        return pltpu.make_async_remote_copy(
-            src_ref=tab.at[who],
-            dst_ref=tab.at[who],
-            send_sem=tab_send.at[0],
-            recv_sem=tab_recv.at[1],
+    def tab_twin(who, late):
+        return pltpu.make_async_remote_copy(
+            src_ref=tab_part(who, late),
+            dst_ref=tab_part(who, late),
+            send_sem=tab_send.at[late, 0],
+            recv_sem=tab_recv.at[late, 1],
             device_id=(sec, partner),
             device_id_type=MESH,
         )
+
+    def tab_take(late):
+        @pl.when(sec > 0)
+        def _():
+            tab_copy(0, late).wait_recv()
+            tab_twin(core, late).start()
+            tab_twin(1 - core, late).wait_recv()
+
+    def tab_pick(here, n):
+        for half in range(2):
+            made = dot(picks, tab[half, :, pl.ds(HALF * n, HALF)], 0, 0)
+            here[:, pl.ds(WIDTH * n + HALF * half, HALF)] = made.astype(BF)
 
     @pl.when(sec == 0)
     def _():
-        for t in range(1, LAYERS):
-            tab_copy(t).start()
+        for late in range(2):
+            for t in range(1, LAYERS):
+                tab_copy(t, late).start()
 
     def gain_copy(d):
         return pltpu.make_async_remote_copy(
@@ -678,23 +694,18 @@
         for t in (1, 3, 2):
             first_copy(t).start()
 
+    launch_flow()
+
     def forward(l, carry):
         here = qkv.at[l]
 
         @pl.when(l == 0)
         def _():
-            @pl.when(sec > 0)
-            def _():
-                tab_copy(0).wait_recv()
-                tab_twin(core).start()
-                tab_twin(1 - core).wait_recv()
-
+            tab_take(0)
             for d in range(1, LAYERS):
                 gain_copy(d).wait_recv()
-            for n in range(3):
-                for half in range(2):
-                    made = dot(picks, tab[half, :, pl.ds(HALF * n, HALF)], 0, 0)
-                    here[:, pl.ds(WIDTH * n + HALF * half, HALF)] = made.astype(BF)
+            for n in range(2):
+                tab_pick(here, n)
 
         @pl.when(l > 0)
         def _():
@@ -703,7 +714,6 @@
 
             @pl.when(l == RING)
             def _():
-                pump(5)
                 settle()
 
             normal, _ = norm_parts(xs[l])
@@ -717,6 +727,8 @@
 
         @pl.when(l == 0)
         def _():
+            tab_take(1)
+            tab_pick(here, 2)
             plane_one(1)
             plane_two(1, 0)
 
@@ -724,8 +736,8 @@
         def _():
             plane_two(2, 0)
 
-        for turn in (1, 2):
-            pl.when(l == turn)(functools.partial(pump, 2 * turn - 1))
+        for turn in range(3):
+            pl.when(l == turn)(functools.partial(pump, 2 * turn + 1))
 
         logits = finish_reduce()
         shifted = jnp.exp(logits - jnp.max(logits, axis=-1, keepdims=True))
@@ -738,10 +750,9 @@
         def _():
             plane_two(1, 1)
             plane_one(2)
-            launch_flow()
-
-        for turn in (1, 2):
-            pl.when(l == turn)(functools.partial(pump, 2 * turn))
+
+        for turn in range(2):
+            pl.when(l == turn)(functools.partial(pump, 2 * turn + 2))
 
         finish_gather(probs_l)
         clear_exchange(probs_l)
@@ -925,12 +936,14 @@
     @pl.when(sec == 0)
     def _():
         for t in range(1, LAYERS):
-            tab_copy(t).wait_send()
+            for late in range(2):
+                tab_copy(t, late).wait_send()
             first_copy(t).wait_send()
 
     @pl.when(sec > 0)
     def _():
-        tab_twin(core).wait_send()
+        for late in range(2):
+            tab_twin(core, late).wait_send()
         first_twin(core).wait_send()
 
     for d in range(1, LAYERS):
@@ -1000,8 +1013,8 @@
             dma((n_row // 2,)),
             dma((2,)),
             dma,
-            dma((LAYERS,)),
-            dma((2,)),
+            dma((2, LAYERS)),
+            dma((2, 2)),
             dma((LAYERS,)),
             dma((LAYERS,)),
             dma((2, LAYERS)),

time: 239 us -> 229 us (0.958)
  Pallas kernels: 238 us -> 229 us
    pallas_call x1, Pallas kernels: 237 us -> 227 us  [local(): pl.pallas_call(functools.partial(kernel, n_row, scale), out_shape=(jax.Sh...]
where the time goes in v8:
time: 229 us
  Pallas kernels  229 us (100%)
    pallas_call x1, Pallas kernels, local(): pl.pallas_call(functools.partial(kernel, n_row, scale), out_shape=(jax.Sh...  227 us

profile of v8, /device:TPU:0, one launch (start us, length us, event | category | flops | bytes accessed | tf_op | source)
XLA Modules:
  0.0 229.3 jit_solution(9853025838668090390)
XLA Ops:
  0.6 226.9 %shard_map.85 = (f32[1,24,2304]{2,1,0:T(8,128)}, f32[1,24,768]{2,1,0:T(8,128)}, f32[1,24]{1,0:T(1,128)}) custom-call(s32[4,2,128]{2,1,0:T(2,128)} %tok_ref.1, bf16[33,768]{1,0:T(8,128)(2,1)} %emb_ref.1, f32[1,768]{1,0:T(1,128)} %gain_ref.1, bf16[4,2,96,2304]{3,2,1,0:T(8,128)(2,1)} %bitcast.3, bf16[4,2,96,768]{3,2,1,0:T(8,128)(2,1)} %bitcast.5, ...), custom_call_target="tpu_custom_call" | custom-call | tf_op jit(solution)/shard_map/pallas_call | solution.py:970
  227.6 1.7 shard_map.86

commit v9 on v8

--- a/solution.py
+++ b/solution.py
@@ -536,6 +536,9 @@
         for d in reversed(range(1, n_chip)):
             ag_copy(buf, d).start()
         hand_copy(buf, 0).start()
+        for d in range(1, n_chip):
+            rs_copy(d).wait_send()
+        level_copy().wait_send()
 
     def finish_gather(buf):
         for d in range(1, n_chip):
@@ -548,9 +551,7 @@
         for d in range(n_chip):
             hand_copy(buf, d).wait_send()
         for d in range(1, n_chip):
-            rs_copy(d).wait_send()
             ag_copy(buf, d).wait_send()
-        level_copy().wait_send()
 
     def halves(ref, base, p):
         cols = pl.ds(base + SEQ * p, SEQ)

time: 229 us -> 229 us (level)
  no operation moved by 1% of the time
where the time goes in v9:
time: 229 us
  Pallas kernels  228 us (100%)
    pallas_call x1, Pallas kernels, local(): pl.pallas_call(functools.partial(kernel, n_row, scale), out_shape=(jax.Sh...  227 us

profile of v9, /device:TPU:0, one launch (start us, length us, event | category | flops | bytes accessed | tf_op | source)
XLA Modules:
  0.0 229.1 jit_solution(5379382682288791475)
XLA Ops:
  0.6 226.8 %shard_map.85 = (f32[1,24,2304]{2,1,0:T(8,128)}, f32[1,24,768]{2,1,0:T(8,128)}, f32[1,24]{1,0:T(1,128)}) custom-call(s32[4,2,128]{2,1,0:T(2,128)} %tok_ref.1, bf16[33,768]{1,0:T(8,128)(2,1)} %emb_ref.1, f32[1,768]{1,0:T(1,128)} %gain_ref.1, bf16[4,2,96,2304]{3,2,1,0:T(8,128)(2,1)} %bitcast.3, bf16[4,2,96,768]{3,2,1,0:T(8,128)(2,1)} %bitcast.5, ...), custom_call_target="tpu_custom_call" | custom-call | tf_op jit(solution)/shard_map/pallas_call | solution.py:971
  227.4 1.7 shard_map.86
